TPU v7x, 32 devices: a whole 2x2x4 slice. The times are simulated.
32 devices in a mesh: fsdp: 8 (over y, x, core), cp: 4 (over z).
Axes of the slice: x: 2, y: 2, z: 4, core: 2. Of those that a mesh axis runs over, the one named last changes fastest.
Arguments:
- hidden: float32 [8, 512, 1536], P('fsdp', 'cp'), may hold values from -6 to 6
- d_out: float32 [8, 512, 1536], P('fsdp', 'cp'), may hold values from -6 to 6
- seg_ids: int32 [8, 512], P('fsdp', 'cp'), may hold values from 0 to 3, never falling along the last dimension, each value on 1 to 256 neighbouring positions
- w_in: bfloat16 [2, 1536, 6448], P(None, 'fsdp', 'cp'), may hold values from -0.15625 to 0.15625
- w_out: bfloat16 [2, 3072, 1536], P(None, 'fsdp', 'cp'), may hold values from -0.109375 to 0.109375
- norm_in: float32 [2, 1536], replicated, may hold values from 0.5 to 1.5
- norm_gate: float32 [2, 3072], replicated, may hold values from 0.5 to 1.5
- conv_w: float32 [2, 4, 3328], replicated, may hold values from -3 to 3
- conv_b: float32 [2, 3328], replicated, may hold values from -2 to 2
- dt_bias: float32 [2, 48], replicated, may hold values from -2 to 0
- a_log: float32 [2, 48], replicated, may hold values from -5.8 to -1.9
- d_skip: float32 [2, 48], replicated, may hold values from 0.5 to 1.5
Outputs:
- activations: float32 [8, 512, 1536], P('fsdp', 'cp')
- d_hidden: float32 [8, 512, 1536], P('fsdp', 'cp')
- grad_w_in: float32 [2, 1536, 6448], P(None, 'fsdp', 'cp')
- grad_w_out: float32 [2, 3072, 1536], P(None, 'fsdp', 'cp')
- grad_norm_in: float32 [2, 1536], replicated
- grad_norm_gate: float32 [2, 3072], replicated
- grad_conv_w: float32 [2, 4, 3328], replicated
- grad_conv_b: float32 [2, 3328], replicated
- grad_dt_bias: float32 [2, 48], replicated
- grad_a_log: float32 [2, 48], replicated
- grad_d_skip: float32 [2, 48], replicated
Inputs may be any that keep to these rules, and one draw needn't show every extreme that they name: `seg_ids`: within each sequence the ids never fall; each id marks one document of at most half of 512 tokens, and every id appears.
All inputs are finite; a program needn't handle non-finite values.
Results may differ from a plain program's by a relative error of at most 0.0093.
Values may be sent and summed in bfloat16 or wider, within the bound.
No kernel may reach another device: no remote copies, remote signals or barrier semaphores. Data moves between devices by JAX's collectives and lax.ppermute only.
A program may use at most 320 MiB of HBM per device.

v0:
```python
import jax
import jax.numpy as jnp
from jax import lax
from jax.sharding import PartitionSpec as P

HEADS = 48
HEADDIM = 64
STATE = 128
CONV = 4
LAYERS = 2
INNER = 3072
CHANNELS = 3328
PROJ = 6448
GROUP = 128


EPSILON = 1e-05
FULL = lax.Precision.HIGHEST


def shifted(block, axis, distance):
    devices = range(lax.axis_size(axis))
    route = [(i - distance, i) for i in devices if i - distance in devices]
    return lax.ppermute(block, axis, route)


def entering(part, axis, combine, identity, reverse):
    count = lax.axis_size(axis)
    place = lax.axis_index(axis)
    ahead = count - 1 - place if reverse else place
    gathered = jax.tree.map(lambda a: lax.all_gather(a, axis), part)
    state = jax.tree.map(lambda a, e: jnp.zeros_like(a) + jnp.asarray(e, a.dtype), part, identity)

    def one(lap, state):
        source = count - 1 - lap if reverse else lap
        return combine(
            state, jax.tree.map(lambda a: lax.dynamic_index_in_dim(a, source, 0, False), gathered)
        )

    return lax.fori_loop(0, ahead, one, state)


def rms_norm(values, gain_vec):
    return (
        values * lax.rsqrt(jnp.mean(values * values, axis=-1, keepdims=True) + EPSILON) * gain_vec
    )


def conv_mix(padded, seg_pad, weight_taps, bias_vec):
    count_rows = padded.shape[-2] - CONV + 1
    target = seg_pad[..., CONV - 1 :]
    summed = bias_vec
    for offset in range(CONV):
        window = padded[..., offset : offset + count_rows, :]
        match_mask = (seg_pad[..., offset : offset + count_rows] == target).astype(jnp.float32)
        summed = summed + weight_taps[offset] * window * match_mask[..., None]
    return jax.nn.silu(summed)


def group_step(decay_rate, carried, block_in):
    state_now, prev_seg = carried
    inputs, step_size, b_rows, c_rows, seg_now = block_in
    length_now = seg_now.shape[0]
    cumul = jnp.cumsum(step_size * decay_rate, axis=0)
    positions = jnp.arange(length_now)
    same_seg = jnp.logical_and(
        seg_now[:, None] == seg_now[None, :], positions[:, None] >= positions[None, :]
    ).astype(jnp.float32)[:, :, None]
    spread = cumul[:, None, :] - cumul[None, :, :]
    lower_mask = jnp.exp(jnp.where(same_seg > 0, spread, 0.0)) * same_seg
    scores = jnp.dot(c_rows, b_rows.T, precision=FULL)
    mixing = scores[:, :, None] * lower_mask * step_size[None, :, :]
    within = jnp.einsum("tsh,shp->thp", mixing, inputs, precision=FULL)
    keep_mask = (seg_now == prev_seg).astype(jnp.float32)
    into_scale = jnp.exp(cumul) * keep_mask[:, None]
    carried_out = (
        jnp.einsum("tn,hpn->thp", c_rows, state_now, precision=FULL) * into_scale[:, :, None]
    )
    tail_mask = (seg_now == seg_now[-1]).astype(jnp.float32)
    weight_s = jnp.exp(cumul[-1][None, :] - cumul) * tail_mask[:, None] * step_size
    fresh = jnp.einsum("shp,sn->hpn", inputs * weight_s[:, :, None], b_rows, precision=FULL)
    new_state = state_now * (jnp.exp(cumul[-1]) * keep_mask[-1])[:, None, None] + fresh
    return ((new_state, seg_now[-1]), within + carried_out)


def ssd_scan(inputs, step_size, decay_rate, b_rows, c_rows, seg_now, prev_seg):
    total_len = seg_now.shape[0]
    blocks = total_len // GROUP

    def advance(carried, block_in):
        return jax.checkpoint(group_step)(decay_rate, carried, block_in)

    shaped = (
        inputs.reshape(blocks, GROUP, HEADS, HEADDIM),
        step_size.reshape(blocks, GROUP, HEADS),
        b_rows.reshape(blocks, GROUP, STATE),
        c_rows.reshape(blocks, GROUP, STATE),
        seg_now.reshape(blocks, GROUP),
    )
    zero_state = jnp.zeros((HEADS, HEADDIM, STATE), jnp.float32)
    final_carry, outputs = lax.scan(advance, (zero_state, prev_seg), shaped)
    return (outputs.reshape(total_len, HEADS, HEADDIM), final_carry[0])


def section_one(
    xbc_raw, dt_raw, prev_rows, conv_w, conv_b, dt_bias, a_log, d_skip, prev_seg, seg_f
):
    seq_count, seq_len = seg_f.shape
    padded = jnp.concatenate([prev_rows, xbc_raw], axis=1)
    seg_pad = jnp.concatenate([prev_seg, seg_f], axis=1)
    mixed = conv_mix(padded, seg_pad, conv_w, conv_b)
    inputs = mixed[..., :INNER].reshape(seq_count, seq_len, HEADS, HEADDIM)
    b_rows = mixed[..., INNER : INNER + STATE]
    c_rows = mixed[..., INNER + STATE :]
    step_size = jax.nn.softplus(dt_raw + dt_bias)
    decay_rate = -jnp.exp(a_log)
    last_prev = prev_seg[:, -1]
    outputs, final_state = jax.vmap(ssd_scan, in_axes=(0, 0, None, 0, 0, 0, 0))(
        inputs, step_size, decay_rate, b_rows, c_rows, seg_f, last_prev
    )
    cumul = jnp.cumsum(step_size * decay_rate, axis=1)
    keep_mask = (seg_f == last_prev[:, None]).astype(jnp.float32)
    into_scale = jnp.exp(cumul) * keep_mask[..., None]
    total_decay = into_scale[:, -1, :]
    local_out = outputs + d_skip[:, None] * inputs
    return (local_out, final_state, total_decay, into_scale, c_rows)


def with_state(local_out, into_scale, c_rows, state_in):
    carried_out = (
        jnp.einsum("btn,bhpn->bthp", c_rows, state_in, precision=FULL) * into_scale[..., None]
    )
    return local_out + carried_out


def ssd_core(
    xbc_raw, dt_raw, prev_rows, conv_w, conv_b, dt_bias, a_log, d_skip, prev_seg, seg_f, state_in
):
    local_out, final_state, total_decay, into_scale, c_rows = section_one(
        xbc_raw, dt_raw, prev_rows, conv_w, conv_b, dt_bias, a_log, d_skip, prev_seg, seg_f
    )
    return (
        with_state(local_out, into_scale, c_rows, state_in),
        final_state,
        total_decay,
        into_scale,
        c_rows,
    )


def gate_norm(ssd_out, gate_z, norm_gate):
    flat_out = ssd_out.reshape(gate_z.shape) * jax.nn.silu(gate_z)
    return rms_norm(flat_out, norm_gate)


def combine(earlier, later):
    decay_early, state_early = earlier
    decay_late, state_late = later
    return (decay_early * decay_late, decay_late[:, :, None, None] * state_early + state_late)


def split_project(project):
    return (
        project[..., :INNER],
        project[..., INNER : INNER + CHANNELS],
        project[..., INNER + CHANNELS :],
    )


def body(
    hidden, d_out, seg_ids, w_in, w_out, norm_in, norm_gate, conv_w, conv_b, dt_bias, a_log, d_skip
):
    seq_count, seq_len, width = hidden.shape
    flat_rows = seq_count * seq_len
    edge = CONV - 1
    seg_f = seg_ids.astype(jnp.float32)
    current = hidden.reshape(flat_rows, width)
    saved = []
    for layer_index in range(LAYERS):
        cols_in, cols_out = (
            lax.all_gather(w_in[layer_index], "cp", axis=1, tiled=True),
            lax.all_gather(w_out[layer_index], "cp", axis=1, tiled=True),
        )
        full_in, full_out = (
            lax.all_gather(cols_in, "fsdp", axis=0, tiled=True),
            lax.all_gather(cols_out, "fsdp", axis=0, tiled=True),
        )
        normed = rms_norm(current, norm_in[layer_index]).astype(jnp.bfloat16)
        project = jnp.dot(normed, full_in, preferred_element_type=jnp.float32).reshape(
            seq_count, seq_len, PROJ
        )
        gate_z, xbc_raw, dt_raw = split_project(project)
        prev_rows, prev_seg = shifted(
            (xbc_raw[:, seq_len - edge :, :], seg_f[:, seq_len - edge :]), "cp", 1
        )
        local_out, final_state, total_decay, into_scale, c_rows = section_one(
            xbc_raw,
            dt_raw,
            prev_rows,
            conv_w[layer_index],
            conv_b[layer_index],
            dt_bias[layer_index],
            a_log[layer_index],
            d_skip[layer_index],
            prev_seg,
            seg_f,
        )
        passed = entering(
            (total_decay, final_state),
            "cp",
            combine,
            (jnp.ones_like(total_decay), jnp.zeros_like(final_state)),
            False,
        )
        state_in = passed[1]
        ssd_out = with_state(local_out, into_scale, c_rows, state_in)
        gated = (
            gate_norm(ssd_out, gate_z, norm_gate[layer_index])
            .astype(jnp.bfloat16)
            .reshape(flat_rows, INNER)
        )
        branch = jnp.dot(gated, full_out, preferred_element_type=jnp.float32)
        saved.append((current, project, prev_rows, prev_seg, state_in))
        current = current + branch
    activations = current.reshape(seq_count, seq_len, width)
    grad_rows = d_out.reshape(flat_rows, width)
    grad_lists = [[None] * LAYERS for column in range(9)]
    for layer_index in reversed(range(LAYERS)):
        current_in, project, prev_rows, prev_seg, state_in = saved[layer_index]
        back_in, back_out = (
            lax.all_gather(w_in[layer_index], "cp", axis=1, tiled=True),
            lax.all_gather(w_out[layer_index], "cp", axis=1, tiled=True),
        )
        full_in, full_out = (
            lax.all_gather(back_in, "fsdp", axis=0, tiled=True),
            lax.all_gather(back_out, "fsdp", axis=0, tiled=True),
        )
        grad_branch = grad_rows.astype(jnp.bfloat16)
        normed_full, norm_pull = jax.vjp(rms_norm, current_in, norm_in[layer_index])
        normed = normed_full.astype(jnp.bfloat16)
        gate_z, xbc_raw, dt_raw = split_project(project)

        def core_local(xbc_in, dt_in, rows_in, taps_in, cbias_in, dtb_in, alog_in, skip_in):
            return ssd_core(
                xbc_in,
                dt_in,
                rows_in,
                taps_in,
                cbias_in,
                dtb_in,
                alog_in,
                skip_in,
                prev_seg,
                seg_f,
                state_in,
            )

        core_out, core_pull = jax.vjp(
            core_local,
            xbc_raw,
            dt_raw,
            prev_rows,
            conv_w[layer_index],
            conv_b[layer_index],
            dt_bias[layer_index],
            a_log[layer_index],
            d_skip[layer_index],
        )
        ssd_out, final_state, total_decay, into_scale, c_rows = core_out
        gated_full, gate_pull = jax.vjp(gate_norm, ssd_out, gate_z, norm_gate[layer_index])
        gated = gated_full.astype(jnp.bfloat16).reshape(flat_rows, INNER)
        grad_w_out = jnp.dot(gated.T, grad_branch, preferred_element_type=jnp.float32)
        grad_gated = jnp.dot(grad_branch, full_out.T, preferred_element_type=jnp.float32).reshape(
            seq_count, seq_len, INNER
        )
        grad_ssd, grad_z, grad_norm_gate = gate_pull(grad_gated)
        local_grad = jnp.einsum(
            "bthp,btn->bhpn", grad_ssd * into_scale[..., None], c_rows, precision=FULL
        )
        chained = entering(
            (total_decay, local_grad),
            "cp",
            combine,
            (jnp.ones_like(total_decay), jnp.zeros_like(local_grad)),
            True,
        )
        grad_after = chained[1]
        grad_decay = jnp.sum(grad_after * state_in, axis=(2, 3))
        pulled = core_pull(
            (grad_ssd, grad_after, grad_decay, jnp.zeros_like(into_scale), jnp.zeros_like(c_rows))
        )
        grad_xbc, grad_dt, grad_prev, grad_taps, grad_cbias, grad_dtb, grad_alog, grad_skip = pulled
        from_next = shifted(grad_prev, "cp", -1)
        grad_xbc = jnp.concatenate(
            [grad_xbc[:, : seq_len - edge, :], grad_xbc[:, seq_len - edge :, :] + from_next], axis=1
        )
        grad_project = (
            jnp.concatenate([grad_z, grad_xbc, grad_dt], axis=-1)
            .reshape(flat_rows, PROJ)
            .astype(jnp.bfloat16)
        )
        grad_w_in = jnp.dot(normed.T, grad_project, preferred_element_type=jnp.float32)
        grad_normed = jnp.dot(grad_project, full_in.T, preferred_element_type=jnp.float32)
        grad_current, grad_norm_in = norm_pull(grad_normed)
        grad_rows = grad_rows + grad_current
        part_in, part_out = (
            lax.psum_scatter(grad_w_in, "fsdp", scatter_dimension=0, tiled=True),
            lax.psum_scatter(grad_w_out, "fsdp", scatter_dimension=0, tiled=True),
        )
        shard_in, shard_out = (
            lax.psum_scatter(part_in, "cp", scatter_dimension=1, tiled=True),
            lax.psum_scatter(part_out, "cp", scatter_dimension=1, tiled=True),
        )
        summed_small = lax.psum(
            (grad_norm_in, grad_norm_gate, grad_taps, grad_cbias, grad_dtb, grad_alog, grad_skip),
            ("fsdp", "cp"),
        )
        results = (shard_in, shard_out) + tuple(summed_small)
        for column in range(9):
            grad_lists[column][layer_index] = results[column]
    stacked = [jnp.stack(grad_lists[column], axis=0) for column in range(9)]
    return (
        activations,
        grad_rows.reshape(seq_count, seq_len, width),
        stacked[0],
        stacked[1],
        stacked[2],
        stacked[3],
        stacked[4],
        stacked[5],
        stacked[6],
        stacked[7],
        stacked[8],
    )


def solution(mesh):
    in_specs = (
        P("fsdp", "cp", None),
        P("fsdp", "cp", None),
        P("fsdp", "cp"),
        P(None, "fsdp", "cp"),
        P(None, "fsdp", "cp"),
        P(),
        P(),
        P(),
        P(),
        P(),
        P(),
        P(),
    )
    out_specs = (
        P("fsdp", "cp", None),
        P("fsdp", "cp", None),
        P(None, "fsdp", "cp"),
        P(None, "fsdp", "cp"),
        P(),
        P(),
        P(),
        P(),
        P(),
        P(),
        P(),
    )
    return jax.shard_map(body, mesh=mesh, in_specs=in_specs, out_specs=out_specs, check_vma=False)
```

profile of v0, /device:TPU:0, one launch (start us, length us, event | category | flops | bytes accessed | tf_op | source)
XLA Modules:
  0.0 2666.1 jit_solution(14825944772853384602)
XLA Ops:
  12.5 123.2 %all-gather.25.cloned.1.call-done = bf16[1,192,6448]{1,0,2:T(2,128)(2,1)} async-done(((bf16[1,192,1612]{1,0,2:T(2,128)(2,1)}), bf16[1,192,6448]{1,0,2:T(2,128)(2,1)}) %all-gather.25.cloned.1.call-update) | async-done | bytes 2476048 | tf_op jit(solution)/shard_map/all_gather | solution.py:181
  135.8 14.3 copy.935
  163.4 88.6 %all-gather.27.cloned.1.call-done = bf16[1,1536,6448]{2,1,0:T(8,128)(2,1)} async-done(((bf16[1,192,6448]{2,1,0:T(8,128)(2,1)}), bf16[1,1536,6448]{2,1,0:T(8,128)(2,1)}) %all-gather.27.cloned.1.call-update) | async-done | bytes 19808272 | tf_op jit(solution)/shard_map/all_gather | solution.py:185
  252.0 12.4 fusion.16
  283.2 14.2 fusion.302
  308.9 97.5 %all-gather.35.cloned.1.call-done = bf16[1,192,6448]{1,0,2:T(2,128)(2,1)} async-done(((bf16[1,192,1612]{1,0,2:T(2,128)(2,1)}), bf16[1,192,6448]{1,0,2:T(2,128)(2,1)}) %all-gather.35.cloned.1.call-update) | async-done | bytes 2476048 | tf_op jit(solution)/shard_map/all_gather | solution.py:181
  406.5 14.5 copy.953
  453.5 68.0 %all-gather.29.cloned.1.call-done = f32[192,64,128]{2,1,0:T(8,128)} async-done(((f32[48,64,128]{2,1,0:T(8,128)}), f32[192,64,128]{2,1,0:T(8,128)}) %all-gather.29.cloned.1.call-update) | async-done | bytes 6291472 | tf_op jit(solution)/shard_map/all_gather | solution.py:31
  533.1 47.0 %all-gather.33.cloned.1.call-done = bf16[1,3072,1536]{2,1,0:T(8,128)(2,1)} async-done(((bf16[1,384,1536]{2,1,0:T(8,128)(2,1)}), bf16[1,3072,1536]{2,1,0:T(8,128)(2,1)}) %all-gather.33.cloned.1.call-update) | async-done | bytes 9437200 | tf_op jit(solution)/shard_map/all_gather | solution.py:186
  585.4 100.8 %all-gather.37.cloned.1.call-done = bf16[1,1536,6448]{2,1,0:T(8,128)(2,1)} async-done(((bf16[1,192,6448]{2,1,0:T(8,128)(2,1)}), bf16[1,1536,6448]{2,1,0:T(8,128)(2,1)}) %all-gather.37.cloned.1.call-update) | async-done | bytes 19808272 | tf_op jit(solution)/shard_map/all_gather | solution.py:185
  686.2 12.4 fusion.19
  718.4 14.6 fusion.300
  753.9 9.8 all_gather.77
  775.3 82.7 %all-gather.39.cloned.1.call-done = f32[192,64,128]{2,1,0:T(8,128)} async-done(((f32[48,64,128]{2,1,0:T(8,128)}), f32[192,64,128]{2,1,0:T(8,128)}) %all-gather.39.cloned.1.call-update) | async-done | bytes 6291472 | tf_op jit(solution)/shard_map/all_gather | solution.py:31
  874.4 42.2 %all-gather.43.cloned.1.call-done = bf16[1,3072,1536]{2,1,0:T(8,128)(2,1)} async-done(((bf16[1,384,1536]{2,1,0:T(8,128)(2,1)}), bf16[1,3072,1536]{2,1,0:T(8,128)(2,1)}) %all-gather.43.cloned.1.call-update) | async-done | bytes 9437200 | tf_op jit(solution)/shard_map/all_gather | solution.py:186
  969.6 89.7 %all-gather.45.cloned.1.call-done = f32[192,64,128]{2,1,0:T(8,128)} async-done(((f32[48,64,128]{2,1,0:T(8,128)}), f32[192,64,128]{2,1,0:T(8,128)}) %all-gather.45.cloned.1.call-update) | async-done | bytes 6291472 | tf_op jit(solution)/shard_map/all_gather | solution.py:31
  1120.0 20.2 multiply_reduce_fusion.4
  1171.7 10.9 multiply_reduce_fusion.21
  1212.1 12.1 fusion.208
  1233.6 15.8 fusion.219
  1269.8 57.7 %all-gather.47.cloned.1.call-done = f32[192,64,128]{2,1,0:T(8,128)} async-done(((f32[48,64,128]{2,1,0:T(8,128)}), f32[192,64,128]{2,1,0:T(8,128)}) %all-gather.47.cloned.1.call-update) | async-done | bytes 6291472 | tf_op jit(solution)/shard_map/all_gather | solution.py:31
  1350.2 10.4 fusion.80
  1395.2 19.2 multiply_reduce_fusion.8
  1441.9 16.1 fusion.71
  1471.6 15.0 multiply_reduce_fusion.22
  1487.8 98.0 %reduce-scatter.13.cloned.1.call-done = f32[384,1536]{1,0:T(8,128)} async-done(((f32[3072,1536]{1,0:T(8,128)}), f32[384,1536]{1,0:T(8,128)}) %reduce-scatter.13.cloned.1.call-update) | async-done | bytes 2359312 | tf_op jit(solution)/shard_map/reduce_scatter | solution.py:308
  1585.8 239.7 %reduce-scatter.11.cloned.1.call-done = f32[192,6448]{1,0:T(8,128)} async-done(((f32[1536,6448]{1,0:T(8,128)}), f32[192,6448]{1,0:T(8,128)}) %reduce-scatter.11.cloned.1.call-update) | async-done | bytes 4952080 | tf_op jit(solution)/shard_map/reduce_scatter | solution.py:307
  1825.5 239.7 %reduce-scatter.9.cloned.1.call-done = f32[192,6448]{1,0:T(8,128)} async-done(((f32[1536,6448]{1,0:T(8,128)}), f32[192,6448]{1,0:T(8,128)}) %reduce-scatter.9.cloned.1.call-update) | async-done | bytes 4952080 | tf_op jit(solution)/shard_map/reduce_scatter | solution.py:307
  2074.4 134.6 %all-reduce.35.cloned.1.call-done = (f32[1,1536]{1,0:T(1,128)}, f32[1,1536]{1,0:T(1,128)}, f32[1,3072]{1,0:T(1,128)}, f32[1,3072]{1,0:T(1,128)}, f32[1,4,3328]{2...) async-done(((f32[1,1536]{1,0:T(1,128)}, f32[1,1536]{1,0:T(1,128)}, ...) | async-done | bytes 171152 | tf_op jit(solution)/shard_map/psum | solution.py:314
  2217.0 42.9 %reduce-scatter.19.cloned.1.call-done = f32[384,384]{1,0:T(8,128)} async-done(((f32[384,1536]{1,0:T(8,128)}), f32[384,384]{1,0:T(8,128)}) %reduce-scatter.19.cloned.1.call-update) | async-done | bytes 589840 | tf_op jit(solution)/shard_map/reduce_scatter | solution.py:312
  2259.9 49.4 %reduce-scatter.15.cloned.1.call-done = f32[384,384]{1,0:T(8,128)} async-done(((f32[384,1536]{1,0:T(8,128)}), f32[384,384]{1,0:T(8,128)}) %reduce-scatter.15.cloned.1.call-update) | async-done | bytes 589840 | tf_op jit(solution)/shard_map/reduce_scatter | solution.py:312
  2311.7 343.2 %all-reduce.37.cloned.1.call-done = (f32[192,6448]{1,0:T(8,128)}, f32[192,6448]{1,0:T(8,128)}) async-done(((f32[192,6448]{1,0:T(8,128)}, f32[192,6448]{1,0:T(8,128)}), (f32[192,6448]{1,0:T(8,128)}, f32[192,6448]{1,0:T(8,128)})) %all-reduce.37.cloned.1.call-update) | async-done | bytes 9904144
  (758 shorter events, 505.3 us)
Async XLA Ops:
  7.2 128.6 %all-gather.25.cloned.1.call-start = ((), (), s32[]{:S(2)}) async-start(), calls=%async_computation.12 | async-start | bytes 8253440 | tf_op jit(solution)/shard_map/all_gather | solution.py:181
  12.5 239.6 %all-gather.27.cloned.1.call-start = ((), (), s32[]{:S(2)}) async-start(), calls=%async_computation.13 | async-start | bytes 22560768 | tf_op jit(solution)/shard_map/all_gather | solution.py:185
  150.1 158.3 %all-gather.31.cloned.1.call-start = ((), (), s32[]{:S(2)}) async-start(), calls=%async_computation.15 | async-start | bytes 1474560 | tf_op jit(solution)/shard_map/all_gather | solution.py:182
  152.0 254.4 %all-gather.35.cloned.1.call-start = ((), (), s32[]{:S(2)}) async-start(), calls=%async_computation.17 | async-start | bytes 8253440 | tf_op jit(solution)/shard_map/all_gather | solution.py:181
  152.2 8.8 collective-permute-start.1
  157.5 364.0 %all-gather.29.cloned.1.call-start = ((), (), s32[]{:S(2)}) async-start(), calls=%async_computation.14 | async-start | bytes 7864320 | tf_op jit(solution)/shard_map/all_gather | solution.py:31
  158.2 528.0 %copy-start.93 = (f32[1536]{0:T(1024)}, f32[1536]{0:T(1024)S(1)}, u32[]{:S(2)}) copy-start(f32[1536]{0:T(1024)S(1)} %get-tuple-element.793) | copy-start | bytes 18436
  159.2 123.9 %copy-start.112 = (f32[3328]{0:T(1024)}, f32[3328]{0:T(1024)S(1)}, u32[]{:S(2)}) copy-start(f32[3328]{0:T(1024)S(1)} %get-tuple-element.787) | copy-start | bytes 39940
  159.2 123.9 %copy-start.114 = (f32[3328]{0:T(1024)}, f32[3328]{0:T(1024)S(1)}, u32[]{:S(2)}) copy-start(f32[3328]{0:T(1024)S(1)} %get-tuple-element.788) | copy-start | bytes 39940
  162.8 260.9 %copy-start.173 = (f32[1,128]{1,0:T(1,128)}, f32[1,128]{1,0:T(1,128)S(1)}, u32[]{:S(2)}) copy-start(f32[1,128]{1,0:T(1,128)S(1)} %get-tuple-element.949) | copy-start | bytes 1540
  266.8 16.3 collective-permute-start
  271.7 161.3 %copy-start.77 = (f32[1,128,48]{2,1,0:T(8,128)}, f32[1,128,48]{2,1,0:T(8,128)S(1)}, u32[]{:S(2)}) copy-start(f32[1,128,48]{2,1,0:T(8,128)S(1)} %reduce_window_sum.91) | copy-start | bytes 73732
  305.7 140.0 %copy-start.71 = (f32[1,128,128]{2,0,1:T(1,128)}, f32[1,128,128]{2,0,1:T(1,128)S(1)}, u32[]{:S(2)}) copy-start(f32[1,128,128]{2,0,1:T(1,128)S(1)} %get-tuple-element.555) | copy-start | bytes 196612
  308.3 271.8 %all-gather.33.cloned.1.call-start = ((), (), s32[]{:S(2)}) async-start(), calls=%async_computation.16 | async-start | bytes 10616832 | tf_op jit(solution)/shard_map/all_gather | solution.py:186
  308.9 377.3 %all-gather.37.cloned.1.call-start = ((), (), s32[]{:S(2)}) async-start(), calls=%async_computation.18 | async-start | bytes 22560768 | tf_op jit(solution)/shard_map/all_gather | solution.py:185
  421.0 323.1 %all-gather.41.cloned.1.call-start = ((), (), s32[]{:S(2)}) async-start(), calls=%async_computation.20 | async-start | bytes 1474560 | tf_op jit(solution)/shard_map/all_gather | solution.py:182
  421.7 436.2 %all-gather.39.cloned.1.call-start = ((), (), s32[]{:S(2)}) async-start(), calls=%async_computation.19 | async-start | bytes 7864320 | tf_op jit(solution)/shard_map/all_gather | solution.py:31
  703.6 14.9 collective-permute-start.2
  708.6 362.0 %copy-start.74 = (f32[1,128,48]{2,1,0:T(8,128)}, f32[1,128,48]{2,1,0:T(8,128)S(1)}, u32[]{:S(2)}) copy-start(f32[1,128,48]{2,1,0:T(8,128)S(1)} %get-tuple-element.536) | copy-start | bytes 73732
  744.0 172.7 %all-gather.43.cloned.1.call-start = ((), (), s32[]{:S(2)}) async-start(), calls=%async_computation.21 | async-start | bytes 10616832 | tf_op jit(solution)/shard_map/all_gather | solution.py:186
  744.6 314.8 %all-gather.45.cloned.1.call-start = ((), (), s32[]{:S(2)}) async-start(), calls=%async_computation.22 | async-start | bytes 7864320 | tf_op jit(solution)/shard_map/all_gather | solution.py:31
  943.9 383.6 %all-gather.47.cloned.1.call-start = ((), (), s32[]{:S(2)}) async-start(), calls=%async_computation.23 | async-start | bytes 7864320 | tf_op jit(solution)/shard_map/all_gather | solution.py:31
  1153.6 8.4 collective-permute-start.3
  1211.8 275.4 %reduce-scatter.17.cloned.1.call-start = ((), (), s32[]{:S(2)}) async-start(), calls=%async_computation.10 | async-start | bytes 21233664 | tf_op jit(solution)/shard_map/reduce_scatter | solution.py:308
  1224.2 361.6 %reduce-scatter.13.cloned.1.call-start = ((), (), s32[]{:S(2)}) async-start(), calls=%async_computation.8 | async-start | bytes 21233664 | tf_op jit(solution)/shard_map/reduce_scatter | solution.py:308
  1232.2 593.3 %reduce-scatter.11.cloned.1.call-start = ((), (), s32[]{:S(2)}) async-start(), calls=%async_computation.7 | async-start | bytes 45121536 | tf_op jit(solution)/shard_map/reduce_scatter | solution.py:307
  1249.4 815.8 %reduce-scatter.9.cloned.1.call-start = ((), (), s32[]{:S(2)}) async-start(), calls=%async_computation.6 | async-start | bytes 45121536 | tf_op jit(solution)/shard_map/reduce_scatter | solution.py:307
  1422.9 12.4 collective-permute-start.4
  1458.1 750.9 %all-reduce.35.cloned.1.call-start = ((), (), s32[]{:S(2)}) async-start(), calls=%async_computation.24 | async-start | bytes 346112 | tf_op jit(solution)/shard_map/psum | solution.py:314
  1487.2 772.8 %reduce-scatter.19.cloned.1.call-start = ((), (), s32[]{:S(2)}) async-start(), calls=%async_computation.11 | async-start | bytes 2949120 | tf_op jit(solution)/shard_map/reduce_scatter | solution.py:312
  1487.8 821.6 %reduce-scatter.15.cloned.1.call-start = ((), (), s32[]{:S(2)}) async-start(), calls=%async_computation.9 | async-start | bytes 2949120 | tf_op jit(solution)/shard_map/reduce_scatter | solution.py:312
  1585.8 1069.1 %all-reduce.37.cloned.1.call-start = ((), (), s32[]{:S(2)}) async-start(), calls=%async_computation.25 | async-start | bytes 20054016
  (216 other events, 3178.2 us)
Sparse Core Ops, SparseCore 0:
  12.6 123.1 all-gather.24
  150.2 101.7 all-gather.26
  254.2 30.1 all-gather.30
  285.8 120.5 all-gather.34
  407.9 113.5 all-gather.28
  523.2 56.8 all-gather.32
  582.6 103.5 all-gather.36
  688.4 30.1 all-gather.40
  744.1 113.8 all-gather.38
  859.7 56.9 all-gather.42
  944.0 115.3 all-gather.44
  1212.0 115.5 all-gather.46
  1331.2 124.6 reduce-scatter.16
  1459.3 126.4 reduce-scatter.12
  1589.3 236.1 reduce-scatter.10
  1829.1 236.1 reduce-scatter.8
  2072.6 136.3 all-reduce.34
  2211.1 48.7 reduce-scatter.18
  2262.2 47.0 reduce-scatter.14
  2311.8 343.0 all-reduce.36
where the time goes:
time: 2680 us; the launch traced here: 2670 us
  waiting for transfers between devices  1950 us (73%)
  matrix products  238 us (9%)
  other arithmetic  223 us (8%)
  local copies, waits for them, and re-layouts  207 us (8%)
    reduce_scatter x2, waiting for transfers between devices, body(): lax.psum_scatter(grad_w_in, 'fsdp', scatter_dimension=0, tiled=True)  479 us
    unnamed x21, waiting for transfers between devices  346 us
    all_gather x4, waiting for transfers between devices, entering(): gathered = jax.tree.map(lambda a: lax.all_gather(a, axis), part)  298 us
    all_gather x2, waiting for transfers between devices, body(): lax.all_gather(w_in[layer_index], 'cp', axis=1, tiled=True)  221 us
    all_gather x2, waiting for transfers between devices, body(): lax.all_gather(cols_in, 'fsdp', axis=0, tiled=True)  189 us
    psum x1, waiting for transfers between devices, body(): lax.psum((grad_norm_in, grad_norm_gate, grad_taps, grad_cbias, grad_dtb,...  135 us
    reduce_scatter x2, waiting for transfers between devices, body(): lax.psum_scatter(grad_w_out, 'fsdp', scatter_dimension=0, tiled=True)  98 us
    reduce_scatter x2, waiting for transfers between devices, body(): lax.psum_scatter(part_out, 'cp', scatter_dimension=1, tiled=True)  92.3 us
  transfers between devices with their start and end apart: 25, of which 17 were waited for; matrix products, arithmetic and copies ran while one was open for 17% of the time, Pallas kernels for 0%

commit v1 on v0

v1 whole, which is shorter than its diff:
```python
import functools

import jax
import jax.numpy as jnp
from jax import lax
from jax.experimental import pallas as pl
from jax.experimental.pallas import tpu as pltpu
from jax.sharding import PartitionSpec as P


HEADS = 48
HEADDIM = 64
STATE = 128
LAYERS = 2
INNER = 3072
CHANNELS = 3328
PROJ = 6448
GROUP = 128
EPSILON = 1e-05
LANES = 128
ROWS = 32

F32 = jnp.float32
BF16 = jnp.bfloat16


def mm(a, b, ca, cb, precision=None):
    return lax.dot_general(
        a, b, (((ca,), (cb,)), ((), ())), precision=precision, preferred_element_type=F32
    )


def parts_of(v):
    high = v.astype(BF16)
    return high, (v - high.astype(F32)).astype(BF16)


def fine(a, b, ca, cb):
    return mm(a[0], b[0], ca, cb) + (mm(a[0], b[1], ca, cb) + mm(a[1], b[0], ca, cb))


def by_mask(v, ex, cb):
    high, low = parts_of(v)
    return mm(high, ex, 1, cb) + mm(low, ex, 1, cb)


def summed_rows(tri, v, ca):
    high = v.astype(BF16)
    rest = v - high.astype(F32)
    middle = rest.astype(BF16)
    low = (rest - middle.astype(F32)).astype(BF16)
    return mm(tri, high, ca, 0) + (mm(tri, middle, ca, 0) + mm(tri, low, ca, 0))


def sigmoid(v):
    return 1.0 / (1.0 + jnp.exp(-v))


def conv_parts(p_ref, prev_ref, ext, meta, cw_ref, hp):
    wide = hp + 2 * STATE
    raw = p_ref[:, hp : hp + wide]
    ext[0:8, :] = prev_ref[:, hp : hp + wide]
    ext[8 : 8 + GROUP, :] = raw
    pre = cw_ref[4:5, :] + cw_ref[3:4, :] * raw
    taps = [raw]
    for back in (1, 2, 3):
        shifted = ext[8 - back : 8 - back + GROUP, :]
        taps.append(shifted)
        pre = pre + cw_ref[3 - back : 4 - back, :] * shifted * meta[:, back - 1 : back]
    return pre, taps


def decay_parts(p_ref, meta, dtp_ref, hp):
    u = p_ref[:, 2 * hp + 2 * STATE :] + dtp_ref[0:1, :]
    dt = jnp.maximum(u, 0.0) + jnp.log1p(jnp.exp(-jnp.abs(u)))
    rows = lax.broadcasted_iota(jnp.int32, (GROUP, GROUP), 0)
    cols = lax.broadcasted_iota(jnp.int32, (GROUP, GROUP), 1)
    lower = rows >= cols
    tri = lower.astype(F32).astype(BF16)
    cum = summed_rows(tri, dt * dtp_ref[1:2, :], 1)
    last = cum[GROUP - 1 : GROUP, :]
    into = jnp.exp(cum) * meta[:, 3:4]
    tail = jnp.exp(last - cum) * meta[:, 4:5]
    through = jnp.exp(last) * meta[0:1, 6:7]
    return u, dt, cum, into, tail, through, lower, tri, rows


def fwd_kernel(
    base_ref, p_ref, prev_ref, meta_ref, seg_ref, cw_ref, dtp_ref, chp_ref, ex_ref,
    rg_ref, y_ref, st_ref, state, ext, *, hp, nh, cps,
):
    j = pl.program_id(0)

    @pl.when(lax.rem(j, cps) == 0)
    def _():
        state[...] = jnp.zeros_like(state)

    meta = meta_ref[...]
    pre, _ = conv_parts(p_ref, prev_ref, ext, meta, cw_ref, hp)
    mixed = pre * sigmoid(pre)
    x = mixed[:, :hp]
    b_rows = parts_of(mixed[:, hp : hp + STATE])
    c_rows = parts_of(mixed[:, hp + STATE :])
    _, dt, cum, into, tail, through, lower, _, _ = decay_parts(p_ref, meta, dtp_ref, hp)
    cum_t = cum.T
    dt_t = dt.T
    scores = fine(c_rows, b_rows, 1, 1)
    same = jnp.logical_and(lower, meta[:, 5:6] == seg_ref[0:1, :])
    ex = ex_ref[...]
    into_x = by_mask(into, ex, 0)
    weight_x = by_mask(tail * dt, ex, 0)
    through_x = by_mask(jnp.broadcast_to(through, (8, LANES)), ex, 0)[0:1, :]
    old = state[...]
    st_ref[0] = old
    carried = fine(c_rows, parts_of(old), 1, 0) * into_x
    state[...] = old * through_x + fine(b_rows, parts_of(x * weight_x), 0, 0)
    low_half = lax.broadcasted_iota(jnp.int32, (GROUP, LANES), 1) < HEADDIM
    total = jnp.zeros((GROUP, LANES), F32)
    for pair in range(nh // 2):
        at = slice(pair * LANES, (pair + 1) * LANES)
        xp = x[:, at]
        xb = parts_of(xp)
        halves = []
        for h in (2 * pair, 2 * pair + 1):
            spread = cum[:, h : h + 1] - cum_t[h : h + 1, :]
            mixing = scores * jnp.exp(jnp.where(same, spread, -1e30)) * dt_t[h : h + 1, :]
            halves.append(fine(parts_of(mixing), xb, 1, 0))
        y = jnp.where(low_half, halves[0], halves[1]) + carried[:, at] + chp_ref[0:1, at] * xp
        y_ref[:, at] = y
        z = p_ref[:, at]
        r = y * (z * sigmoid(z))
        rg_ref[:, at] = (r * chp_ref[1:2, at]).astype(BF16)
        total = total + r * r
    rg_ref[:, hp:] = total.astype(BF16)


def bwd_kernel(
    base_ref, p_ref, prev_ref, meta_ref, seg_ref, cw_ref, dtp_ref, chp_ref, ex_ref,
    y_ref, st_ref, gx_ref,
    gp_ref, gated_ref, gcw_ref, gch_ref, gdt_ref,
    dstate, ext, edge, row_sums, *, hp, nh, cps,
):
    step = pl.program_id(0)
    j = pl.num_programs(0) - 1 - step

    @pl.when(step == 0)
    def _():
        gcw_ref[...] = jnp.zeros_like(gcw_ref)
        gch_ref[...] = jnp.zeros_like(gch_ref)
        gdt_ref[...] = jnp.zeros_like(gdt_ref)
        row_sums[...] = jnp.zeros_like(row_sums)

    @pl.when(lax.rem(j, cps) == cps - 1)
    def _():
        dstate[...] = jnp.zeros_like(dstate)
        edge[...] = jnp.zeros_like(edge)

    meta = meta_ref[...]
    pre, taps = conv_parts(p_ref, prev_ref, ext, meta, cw_ref, hp)
    sig = sigmoid(pre)
    mixed = pre * sig
    x = mixed[:, :hp]
    b_rows = parts_of(mixed[:, hp : hp + STATE])
    c_rows = parts_of(mixed[:, hp + STATE :])
    u, dt, cum, into, tail, through, lower, tri, rows = decay_parts(p_ref, meta, dtp_ref, hp)
    cum_t = cum.T
    dt_t = dt.T
    scores = fine(c_rows, b_rows, 1, 1)
    same = jnp.logical_and(lower, meta[:, 5:6] == seg_ref[0:1, :])
    ex = ex_ref[...]
    weight = tail * dt
    into_x = by_mask(into, ex, 0)
    weight_x = by_mask(weight, ex, 0)
    through_x = by_mask(jnp.broadcast_to(through, (8, LANES)), ex, 0)[0:1, :]

    scal = gx_ref[:, hp:]
    inv = scal[:, 0:1] + scal[:, 1:2]
    pull = (scal[:, 2:3] + scal[:, 3:4]) * inv * inv * (1.0 / INNER)
    low_half = lax.broadcasted_iota(jnp.int32, (GROUP, LANES), 1) < HEADDIM
    lane = lax.broadcasted_iota(jnp.int32, (GROUP, LANES), 1)
    dys = []
    for pair in range(nh // 2):
        at = slice(pair * LANES, (pair + 1) * LANES)
        z, y, g = p_ref[:, at], y_ref[:, at], gx_ref[:, at]
        gain = chp_ref[1:2, at]
        sz = sigmoid(z)
        silu = z * sz
        r = y * silu
        scaled = r * inv
        gated_ref[:, at] = (scaled * gain).astype(BF16)
        gch_ref[1:2, at] += jnp.sum(g * scaled, axis=0, keepdims=True)
        dr = inv * (g * gain) - r * pull
        dys.append(dr * silu)
        gp_ref[:, at] = (dr * y * (sz * (1.0 + z * (1.0 - sz)))).astype(BF16)
    dy = jnp.concatenate(dys, axis=1)

    old = st_ref[0]
    after = dstate[...]
    old_b, after_b = parts_of(old), parts_of(after)
    dxw = fine(b_rows, after_b, 1, 0)
    dx_wide = dxw * weight_x + chp_ref[0:1, :] * dy
    db = fine(parts_of(x * weight_x), after_b, 1, 1)
    dye = parts_of(dy * into_x)
    dc = fine(dye, old_b, 1, 1)
    dweight = by_mask(dxw * x, ex, 1)
    dinto = by_mask(dy * fine(c_rows, old_b, 1, 0), ex, 1)
    dthrough = by_mask(
        jnp.broadcast_to(jnp.sum(old * after, axis=0, keepdims=True), (8, hp)), ex, 1
    )[0:1, :]
    dstate[...] = after * through_x + fine(c_rows, dye, 0, 0)
    gch_ref[0:1, :] += jnp.sum(dy * x, axis=0, keepdims=True)

    dscores = jnp.zeros((GROUP, GROUP), F32)
    row_part = jnp.zeros((GROUP, LANES), F32)
    dx_parts = []
    for pair in range(nh // 2):
        at = slice(pair * LANES, (pair + 1) * LANES)
        xb = parts_of(x[:, at])
        dyb = parts_of(dy[:, at])
        halves = []
        for side in (0, 1):
            h = 2 * pair + side
            mine = low_half if side == 0 else jnp.logical_not(low_half)
            spread = cum[:, h : h + 1] - cum_t[h : h + 1, :]
            decay = jnp.exp(jnp.where(same, spread, -1e30))
            dtr = dt_t[h : h + 1, :]
            decayed = scores * decay
            mixing = parts_of(decayed * dtr)
            dmix = fine([jnp.where(mine, v, jnp.zeros_like(v)) for v in dyb], xb, 1, 1)
            dscores = dscores + dmix * decay * dtr
            flow = dmix * decayed
            row_sums[h : h + 1, :] = jnp.sum(flow, axis=0, keepdims=True)
            across = jnp.sum(flow * dtr, axis=1, keepdims=True)
            row_part = jnp.where(lane == h, across, row_part)
            halves.append(fine(mixing, dyb, 0, 0))
        dx_parts.append(jnp.where(low_half, halves[0], halves[1]))
    dx_wide = dx_wide + jnp.concatenate(dx_parts, axis=1)
    dsb = parts_of(dscores)
    db = db + fine(dsb, c_rows, 0, 0)
    dc = dc + fine(dsb, b_rows, 1, 0)

    col_part = row_sums[...].T
    used = dweight * weight
    at_last = jnp.sum(used, axis=0, keepdims=True) + dthrough * through
    dcum = row_part + dinto * into - dt * col_part - used
    dcum = dcum + jnp.where(rows == GROUP - 1, at_last, 0.0)
    dstep = summed_rows(tri, dcum, 0)
    ddt = col_part + dweight * tail + dstep * dtp_ref[1:2, :]
    du = ddt * sigmoid(u)
    gdt_ref[0:1, :] += jnp.sum(du, axis=0, keepdims=True)
    gdt_ref[1:2, :] += jnp.sum(dstep * dt, axis=0, keepdims=True)
    gp_ref[:, 2 * hp + 2 * STATE :] = du.astype(BF16)

    dmixed = jnp.concatenate([dx_wide, db, dc], axis=1)
    dpre = dmixed * (sig * (1.0 + pre * (1.0 - sig)))
    gcw_ref[4:5, :] += jnp.sum(dpre, axis=0, keepdims=True)
    gcw_ref[3:4, :] += jnp.sum(dpre * taps[0], axis=0, keepdims=True)
    draw = cw_ref[3:4, :] * dpre
    masked_all = []
    for back in (1, 2, 3):
        masked = dpre * meta[:, back - 1 : back]
        gcw_ref[3 - back : 4 - back, :] += jnp.sum(masked * taps[back], axis=0, keepdims=True)
        masked_all.append(masked)
    for back in (1, 2, 3):
        masked = masked_all[back - 1]
        ext[0:GROUP, :] = masked
        ext[GROUP : GROUP + 8, :] = edge[back - 1]
        draw = draw + cw_ref[3 - back : 4 - back, :] * ext[back : back + GROUP, :]
        edge[back - 1] = masked[0:8, :]
    gp_ref[:, hp : 2 * hp + 2 * STATE] = draw.astype(BF16)


def place_of(other, count):
    half = other >> 1
    if count == 8:
        half = half ^ (half >> 1)
    return half + (other & 1) * (count // 2)


def kernel_specs(hp, wid, n, reverse):
    def nat(i):
        return n - 1 - i if reverse else i

    def tok(i, base):
        return (place_of(nat(i) ^ base[0], n), 0)

    def prev(i, base):
        block = place_of(jnp.maximum(nat(i) - 1, 0) ^ base[0], n)
        return (block * (GROUP // 8) + GROUP // 8 - 1, 0)

    def same(i, base):
        return (0, 0)

    shared = [
        pl.BlockSpec((GROUP, wid), tok),
        pl.BlockSpec((8, wid), prev),
        pl.BlockSpec((GROUP, LANES), lambda i, base: (nat(i), 0)),
        pl.BlockSpec((8, GROUP), lambda i, base: (0, nat(i))),
        pl.BlockSpec((8, hp + 2 * STATE), same),
        pl.BlockSpec((8, LANES), same),
        pl.BlockSpec((8, hp), same),
        pl.BlockSpec((LANES, hp), same),
    ]
    state_spec = pl.BlockSpec((1, STATE, hp), lambda i, base: (nat(i), 0, 0))
    return tok, same, shared, state_spec


def ssd_forward(base, project, meta, segs, cw, dtp, chp, ex, *, hp, nh, cps):
    n = project.shape[0] // GROUP
    wid = project.shape[1]
    tok, _, shared, state_spec = kernel_specs(hp, wid, n, False)
    return pl.pallas_call(
        functools.partial(fwd_kernel, hp=hp, nh=nh, cps=cps),
        grid_spec=pltpu.PrefetchScalarGridSpec(
            num_scalar_prefetch=1,
            grid=(n,),
            in_specs=shared,
            out_specs=[
                pl.BlockSpec((GROUP, hp + LANES), tok),
                pl.BlockSpec((GROUP, hp), tok),
                state_spec,
            ],
            scratch_shapes=[
                pltpu.VMEM((STATE, hp), F32),
                pltpu.VMEM((GROUP + 8, hp + 2 * STATE), F32),
            ],
        ),
        out_shape=[
            jax.ShapeDtypeStruct((n * GROUP, hp + LANES), BF16),
            jax.ShapeDtypeStruct((n * GROUP, hp), F32),
            jax.ShapeDtypeStruct((n, STATE, hp), F32),
        ],
        cost_estimate=pl.CostEstimate(flops=10**9, bytes_accessed=4 * 10**7, transcendentals=0),
        name="ssd_forward",
    )(base, project, project, meta, segs, cw, dtp, chp, ex)


def ssd_backward(base, project, meta, segs, cw, dtp, chp, ex, y, states, gx, *, hp, nh, cps):
    n = project.shape[0] // GROUP
    wid = project.shape[1]
    tok, same, shared, state_spec = kernel_specs(hp, wid, n, True)
    wide = hp + 2 * STATE
    return pl.pallas_call(
        functools.partial(bwd_kernel, hp=hp, nh=nh, cps=cps),
        grid_spec=pltpu.PrefetchScalarGridSpec(
            num_scalar_prefetch=1,
            grid=(n,),
            in_specs=shared
            + [
                pl.BlockSpec((GROUP, hp), tok),
                state_spec,
                pl.BlockSpec((GROUP, hp + LANES), tok),
            ],
            out_specs=[
                pl.BlockSpec((GROUP, wid), tok),
                pl.BlockSpec((GROUP, hp), tok),
                pl.BlockSpec((8, wide), same),
                pl.BlockSpec((8, hp), same),
                pl.BlockSpec((8, LANES), same),
            ],
            scratch_shapes=[
                pltpu.VMEM((STATE, hp), F32),
                pltpu.VMEM((GROUP + 8, wide), F32),
                pltpu.VMEM((3, 8, wide), F32),
                pltpu.VMEM((LANES, GROUP), F32),
            ],
        ),
        out_shape=[
            jax.ShapeDtypeStruct((n * GROUP, wid), BF16),
            jax.ShapeDtypeStruct((n * GROUP, hp), BF16),
            jax.ShapeDtypeStruct((8, wide), F32),
            jax.ShapeDtypeStruct((8, hp), F32),
            jax.ShapeDtypeStruct((8, LANES), F32),
        ],
        cost_estimate=pl.CostEstimate(flops=10**9, bytes_accessed=8 * 10**7, transcendentals=0),
        name="ssd_backward",
    )(base, project, project, meta, segs, cw, dtp, chp, ex, y, states, gx)


def pad_to(a, axis, size):
    widths = [(0, 0)] * a.ndim
    widths[axis] = (0, size - a.shape[axis])
    return jnp.pad(a, widths)


def swap(a, axis, bit):
    size = lax.axis_size(axis)
    return lax.ppermute(a, axis, [(i, i ^ bit) for i in range(size)])


def far_first(count):
    return (6, 7, 2, 4, 3, 5, 1) if count == 8 else tuple(range(1, count))


def sum_all(a):
    for axis in ("fsdp", "cp"):
        bit = 1
        while bit < lax.axis_size(axis):
            a = a + swap(a, axis, bit)
            bit *= 2
    return a


def gather_plane(a, beside=()):
    fs = lax.axis_size("fsdp")
    if fs != 8:
        bit = 2
        while bit < fs:
            a = jnp.concatenate([a, swap(a, "fsdp", bit)], axis=0)
            bit *= 2
        return jnp.concatenate([a, swap(a, "fsdp", 1)], axis=0), beside
    half = a.shape[0] // 2
    along_x = swap(a, "fsdp", 2)
    along_y = swap(a, "fsdp", 4)
    mate = swap(a, "fsdp", 1)
    if beside:
        along_x, along_y, *beside = together(along_x, along_y, *beside)
    corner = jnp.concatenate(
        [swap(along_x[:half], "fsdp", 4), swap(along_y[half:], "fsdp", 2)], axis=0
    )
    mate_x = swap(along_x, "fsdp", 1)
    mate_y = swap(along_y, "fsdp", 1)
    mate_c = swap(corner, "fsdp", 1)
    parts = [a, along_x, corner, along_y, mate, mate_x, mate_c, mate_y]
    return jnp.concatenate(parts, axis=0), beside


def scatter_plane(rows, weight, contract, split, beside=(None, None)):
    fs = lax.axis_size("fsdp")
    half = rows.shape[0] // 2
    one, two = beside
    theirs = mm(rows[half:], weight, 1, contract).astype(BF16)
    mate = swap(theirs, "fsdp", 1)
    if one is not None:
        mate, one = together(mate, one)
    total = mm(rows[:half], weight, 1, contract) + mate.astype(F32)
    if fs != 8:
        bit = fs // 2
        while bit > 1:
            half = total.shape[0] // 2
            got = swap(total[half:].astype(BF16), "fsdp", bit)
            total = total[:half] + got.astype(F32)
            bit //= 2
        return total, one, two
    g = GROUP
    sent_x = swap(total[g : 3 * g, :split].astype(BF16), "fsdp", 2)
    sent_y = swap(total[2 * g :, split:].astype(BF16), "fsdp", 4)
    if two is not None:
        sent_x, sent_y, *two = together(sent_x, sent_y, *two)
    turn_y = (total[3 * g :, :split] + sent_x[g:].astype(F32)).astype(BF16)
    turn_x = (total[g : 2 * g, split:] + sent_y[:g].astype(F32)).astype(BF16)
    last_y = swap(turn_y, "fsdp", 4)
    last_x = swap(turn_x, "fsdp", 2)
    left = total[:g, :split] + sent_x[:g].astype(F32) + last_y.astype(F32)
    right = total[:g, split:] + sent_y[g:].astype(F32) + last_x.astype(F32)
    return jnp.concatenate([left, right], axis=1), one, two


def column_pieces(fs, cp):
    heads = HEADS // fs
    hc = heads * HEADDIM
    hp = (heads + heads % 2) * HEADDIM
    shard = PROJ // cp
    pieces = []
    for d in range(fs):
        mine = []
        for start, count, to in (
            (d * hc, hc, 0),
            (INNER + d * hc, hc, hp),
            (2 * INNER, 2 * STATE, 2 * hp),
            (INNER + CHANNELS + d * heads, heads, 2 * hp + 2 * STATE),
        ):
            while count:
                s, at = divmod(start, shard)
                n = min(count, shard - at)
                mine.append((s, at, n, to))
                start, count, to = start + n, count - n, to + n
        pieces.append(mine)
    return pieces


def pack_kernel(tie_ref, got_ref, out_ref, *, pieces):
    def some(k, _):
        rows = pl.ds(pl.multiple_of(k * ROWS, ROWS), ROWS)
        for d, mine in enumerate(pieces):
            out_ref[d, rows, :] = jnp.zeros_like(out_ref[d, rows, :])
            for s, at, n, to in mine:
                out_ref[d, rows, to : to + n] = got_ref[s, rows, at : at + n]
        return 0

    lax.fori_loop(0, got_ref.shape[1] // ROWS, some, 0)


def pack(tie, got, wid, fs, cp):
    return pl.pallas_call(
        functools.partial(pack_kernel, pieces=column_pieces(fs, cp)),
        in_specs=[
            pl.BlockSpec(memory_space=pltpu.SMEM),
            pl.BlockSpec(memory_space=pltpu.VMEM),
        ],
        out_shape=jax.ShapeDtypeStruct((fs, got.shape[1], wid), BF16),
        name="pack_columns",
    )(tie, got)


def unpack_kernel(f_ref, *refs, pieces, common, fs):
    blocks, out_ref, held, sems = refs[:fs], refs[fs], refs[fs + 1], refs[fs + 2]
    f = f_ref[0]
    copies = [
        pltpu.make_async_copy(blocks[r], held.at[f ^ r], sems.at[r]) for r in range(fs)
    ]
    for copy in copies:
        copy.start()
    for copy in copies:
        copy.wait()

    def some(k, _):
        rows = pl.ds(pl.multiple_of(k * ROWS, ROWS), ROWS)
        for d, mine in enumerate(pieces):
            for s, at, n, to in mine:
                if common[0] <= to < common[1]:
                    if d == 0:
                        both = held[0, rows, to : to + n].astype(F32)
                        for e in range(1, fs):
                            both = both + held[e, rows, to : to + n].astype(F32)
                        out_ref[s, rows, at : at + n] = both.astype(BF16)
                else:
                    out_ref[s, rows, at : at + n] = held[d, rows, to : to + n]
        return 0

    lax.fori_loop(0, out_ref.shape[1] // ROWS, some, 0)


def unpack(f, blocks, hp, fs, cp):
    rows, wid = blocks[0].shape
    return pl.pallas_call(
        functools.partial(
            unpack_kernel,
            pieces=column_pieces(fs, cp),
            common=(2 * hp, 2 * hp + 2 * STATE),
            fs=fs,
        ),
        in_specs=[pl.BlockSpec(memory_space=pltpu.SMEM)]
        + [pl.BlockSpec(memory_space=pl.ANY)] * fs,
        out_shape=jax.ShapeDtypeStruct((cp, rows, PROJ // cp), BF16),
        scratch_shapes=[pltpu.VMEM((fs, rows, wid), BF16), pltpu.SemaphoreType.DMA((fs,))],
        name="unpack_columns",
    )(f, *blocks)


def assemble_kernel(f_ref, packed, *refs, order):
    blocks, out_ref, sems = refs[: len(order)], refs[-2], refs[-1]
    f = f_ref[0]
    copies = [pltpu.make_async_copy(packed.at[f], out_ref.at[f], sems.at[0])]
    for k, r in enumerate(order):
        copies.append(pltpu.make_async_copy(blocks[k], out_ref.at[f ^ r], sems.at[k + 1]))
    for copy in copies:
        copy.start()
    for copy in copies:
        copy.wait()


def assemble(f, packed, blocks, order):
    return pl.pallas_call(
        functools.partial(assemble_kernel, order=order),
        in_specs=[pl.BlockSpec(memory_space=pltpu.SMEM)]
        + [pl.BlockSpec(memory_space=pl.ANY)] * (1 + len(blocks)),
        out_specs=pl.BlockSpec(memory_space=pltpu.VMEM),
        out_shape=jax.ShapeDtypeStruct(packed.shape, packed.dtype),
        scratch_shapes=[pltpu.SemaphoreType.DMA((1 + len(blocks),))],
        name="assemble_rows",
    )(f, packed, *blocks)


def together(*values):
    return lax.optimization_barrier(values)


def scale_of(u):
    return lax.rsqrt(jnp.mean(u * u, axis=-1, keepdims=True) + EPSILON)


def split_two(v):
    high = lax.reduce_precision(v, 8, 7)
    return high.astype(BF16), (v - high).astype(BF16)


def steps(
    hidden, d_out, seg_ids, w_in, w_out, norm_in, norm_gate, conv_w, conv_b, dt_bias, a_log, d_skip
):
    fs, cp = lax.axis_size("fsdp"), lax.axis_size("cp")
    f = lax.axis_index("fsdp")
    width = hidden.shape[-1]
    heads = HEADS // fs
    nh = heads + heads % 2
    hc, hp = heads * HEADDIM, nh * HEADDIM
    wid = 2 * hp + 2 * STATE + LANES
    rows_in = width // fs
    cps = cp
    per = fs // cp
    planes = [k // 2 if k % 2 == 0 else cp - 1 - k // 2 for k in range(cp)]
    there = [
        (a * cp + b, ((a // cp) * cp + b) * cp + planes[a % cp])
        for a in range(fs)
        for b in range(cp)
    ]
    back = [(b, a) for a, b in there]
    base = f.astype(jnp.int32).reshape(1)

    def move(a, route):
        return lax.ppermute(a, ("fsdp", "cp"), route)

    first = hidden.reshape(GROUP, width)
    scale = scale_of(first)
    normed = lax.reduce_precision(first * scale * norm_in[0], 8, 7)
    high, low = split_two(1.0 / scale)

    def rebuilt(normed, high, low):
        return normed.astype(F32) * (high.astype(F32) + low.astype(F32)) / norm_in[0]

    left_over = (first - rebuilt(normed, high, low)).astype(BF16)
    normed = normed.astype(BF16)
    marks = pad_to(
        jnp.concatenate([seg_ids.reshape(GROUP, 1).astype(BF16), high, low], axis=1), 1, LANES
    )
    moved = move(jnp.concatenate([normed, marks], axis=1), there)
    left_over = move(left_over, there)
    own_scale = moved[:, width + 1 : width + 3]
    own_normed = moved[:, :width]
    marked, _ = gather_plane(moved)
    normed_all = marked[:, :width]
    marks = marked[:, width].astype(F32).reshape(fs, GROUP)
    natural = [place_of(jnp.asarray(k) ^ f, fs) for k in range(fs)]
    segs = jnp.stack(
        [lax.dynamic_index_in_dim(marks, n, 0, False) for n in natural]
    ).reshape(per, cps * GROUP)
    total = per * cps * GROUP
    place = jnp.arange(cps * GROUP)
    cols = []
    for k in (1, 2, 3):
        before = jnp.roll(segs, k, axis=1)
        cols.append(jnp.logical_and(before == segs, place[None, :] >= k).astype(F32))
    grouped = segs.reshape(per, cps, GROUP)
    before = jnp.concatenate([segs[:, :1], grouped[:, :-1, -1]], axis=1)
    keep = (grouped == before[:, :, None]).astype(F32)
    tail = (grouped == grouped[:, :, -1:]).astype(F32)
    cols += [keep, tail, grouped, jnp.broadcast_to(keep[:, :, -1:], keep.shape)]
    meta = pad_to(jnp.stack([c.reshape(total) for c in cols], axis=1), 1, LANES)
    seg_rows = jnp.broadcast_to(segs.reshape(1, total), (8, total))
    ex = (jnp.arange(hp)[None, :] // HEADDIM == jnp.arange(LANES)[:, None]).astype(BF16)

    eye = jnp.eye(LANES, dtype=BF16)

    def send_in(packed):
        return [
            swap(lax.dynamic_index_in_dim(packed, f ^ r, 0, False), "fsdp", r)
            for r in far_first(fs)
        ]

    def place_in(packed, blocks):
        return assemble(base, packed, blocks, far_first(fs)).reshape(width, wid)

    def finish_out(got):
        out_w = pad_to(got.transpose(1, 0, 2).reshape(hc, width), 0, hp)
        return jnp.concatenate(
            [
                pad_to(out_w, 1, width + LANES),
                jnp.concatenate([jnp.zeros((LANES, width), BF16), eye], axis=1),
            ],
            axis=0,
        )

    def gather_cp(a):
        return lax.all_gather(a, "cp", axis=0)

    got_in, got_out = [None] * LAYERS, [None] * LAYERS
    got_in[0] = gather_cp(w_in[0])
    last_grad = d_out.reshape(GROUP, width)
    packed = pack(jnp.zeros((1,), F32), got_in[0], wid, fs, cp)
    full_in, full_out = [place_in(packed, send_in(packed))], []
    for i in range(LAYERS):
        if i:
            got_in[i] = gather_cp(w_in[i])
        got_out[i] = gather_cp(w_out[i])

    def own(v, size, padded):
        return pad_to(lax.dynamic_slice_in_dim(v, f * size, size, v.ndim - 1), v.ndim - 1, padded)

    params = []
    for i in range(LAYERS):
        taps = jnp.concatenate([conv_w[i], conv_b[i][None]], axis=0)
        cw = jnp.concatenate([own(taps[:, :INNER], hc, hp), taps[:, INNER:]], axis=1)
        rate = -jnp.exp(own(a_log[i], heads, heads))
        dtp = jnp.stack([own(dt_bias[i], heads, LANES), pad_to(rate, 0, LANES)])
        skip = own(jnp.repeat(d_skip[i], HEADDIM), hc, hp)
        chp = jnp.stack([skip, own(norm_gate[i], hc, hp)])
        params.append((pad_to(cw, 0, 8), pad_to(dtp, 0, 8), pad_to(chp, 0, 8), ex))

    saved = []
    sizes = dict(hp=hp, nh=nh, cps=cps)
    added = 0.0
    for i in range(LAYERS):
        if i:
            normed = (current * scale_of(current) * norm_in[i]).astype(BF16)
            normed_all, blocks = gather_plane(normed, blocks)
            full_in.append(place_in(packed, blocks))
        project = mm(normed_all, full_in[i], 1, 0)
        if i + 1 < LAYERS:
            packed = pack(project[0, :1], got_in[i + 1], wid, fs, cp)
            project, packed = together(project, packed)
            blocks = send_in(packed)
        if i + 1 == LAYERS:
            project, last_grad = together(project, last_grad)
            moved_grad = move(last_grad.astype(BF16), there)
        rg, y, states = ssd_forward(base, project, meta, seg_rows, *params[i], **sizes)
        rg, got_out[i] = together(rg, got_out[i])
        full_out.append(finish_out(got_out[i]))
        summed, _, _ = scatter_plane(rg, full_out[i], 0, width // 2)
        inv = lax.rsqrt(
            jnp.sum(summed[:, width:], axis=1, keepdims=True) * (1.0 / INNER) + EPSILON
        )
        branch = summed[:, :width] * inv
        if i == 0:
            current = rebuilt(own_normed, own_scale[:, :1], own_scale[:, 1:]) + left_over
        saved.append((current, normed_all, project, y, states, branch, inv))
        current = current + branch
        added = added + branch
    activations = first + move(added.astype(BF16), back).astype(F32)

    grads_in, grads_out, small = [None] * LAYERS, [None] * LAYERS, [None] * LAYERS
    change = 0.0
    waiting = None

    def send_out(d_wi):
        blocks = {0: lax.dynamic_index_in_dim(d_wi, f, 0, False)}
        for r in far_first(fs):
            blocks[r] = swap(lax.dynamic_index_in_dim(d_wi, f ^ r, 0, False), "fsdp", r)
        return [blocks[r] for r in range(fs)]

    def sum_in(wide):
        wide = lax.psum_scatter(wide, "cp", scatter_dimension=0, tiled=True)
        return wide[0].astype(F32)

    for i in reversed(range(LAYERS)):
        before, normed_all, project, y, states, branch, inv = saved[i]
        grad_b = (moved_grad.astype(F32) + change).astype(BF16)
        dots = jnp.sum(branch * grad_b.astype(F32), axis=1, keepdims=True)
        scal = jnp.concatenate([*split_two(inv), *split_two(dots)], axis=1)
        payload = jnp.concatenate([grad_b, pad_to(scal, 1, LANES)], axis=1)
        if waiting is not None:
            payload, waiting = gather_plane(payload, waiting)
            wide = unpack(base, send_out(waiting[0]), hp, fs, cp)
        else:
            payload, _ = gather_plane(payload)
        gx = mm(payload, full_out[i], 1, 1)
        gp, gated, gcw, gch, gdt = ssd_backward(
            base, project, meta, seg_rows, *params[i], y, states, gx, **sizes
        )
        if waiting is not None:
            gp, wide, grads_out[i + 1] = together(gp, wide, grads_out[i + 1])
            grads_in[i + 1] = sum_in(wide)
        d_wi = mm(normed_all, gp, 0, 0).astype(BF16).reshape(fs, rows_in, wid)
        d_wo = mm(gated[:, :hc], payload[:, :width], 0, 0).astype(BF16)
        if i:
            g_normed, d_wo, waiting = scatter_plane(
                gp, full_in[i], 1, width // 2, (d_wo, [d_wi])
            )
        else:
            gp, d_wi, d_wo = together(gp, d_wi, d_wo)
            blocks = send_out(d_wi)
            g_normed, _, blocks = scatter_plane(gp, full_in[i], 1, width // 2, (None, blocks))
        d_wo = d_wo.reshape(hc, cp, width // cp).transpose(1, 0, 2)
        d_wo = lax.psum_scatter(d_wo, "cp", scatter_dimension=0, tiled=True)
        grads_out[i] = d_wo[0].astype(F32)
        if i == 0:
            wide = unpack(base, blocks, hp, fs, cp)
            wide, grads_in[i + 1] = together(wide, grads_in[i + 1])
            grads_in[i] = sum_in(wide)

        scale = scale_of(before)
        hat = before * scale
        pulled = g_normed * norm_in[i]
        change = change + scale * (pulled - hat * jnp.mean(pulled * hat, axis=-1, keepdims=True))
        g_norm_in = jnp.sum(g_normed * hat, axis=0)

        table = jnp.zeros((8, CHANNELS), F32)
        mine = jnp.concatenate([gcw[:5, :hc], gch[1:2, :hc]], axis=0)
        table = lax.dynamic_update_slice(table, mine, (0, f * hc))
        table = table.at[:5, INNER:].add(gcw[:5, hp:])
        table = table.at[6, :width].set(g_norm_in)
        by_head = jnp.sum(gch[0, :hc].reshape(heads, HEADDIM), axis=1)
        rate = -jnp.exp(own(a_log[i], heads, heads))
        thin = jnp.stack([gdt[0, :heads], gdt[1, :heads] * rate, by_head])
        thin = lax.dynamic_update_slice(jnp.zeros((3, HEADS), F32), thin, (0, f * heads))
        table = table.at[7, : 3 * HEADS].set(thin.reshape(-1))
        small[i] = table

    d_hidden = last_grad + move(change.astype(BF16), back).astype(F32)
    tables = sum_all(jnp.stack(small))
    shape = hidden.shape
    thin = tables[:, 7, : 3 * HEADS].reshape(LAYERS, 3, HEADS)
    return (
        activations.reshape(shape),
        d_hidden.reshape(shape),
        jnp.stack(grads_in),
        jnp.stack(grads_out),
        tables[:, 6, :width],
        tables[:, 5, :INNER],
        tables[:, :4],
        tables[:, 4],
        thin[:, 0],
        thin[:, 1],
        thin[:, 2],
    )


def solution(mesh):
    in_specs = (
        P("fsdp", "cp", None),
        P("fsdp", "cp", None),
        P("fsdp", "cp"),
        P(None, "fsdp", "cp"),
        P(None, "fsdp", "cp"),
    ) + (P(),) * 7
    out_specs = (
        P("fsdp", "cp", None),
        P("fsdp", "cp", None),
        P(None, "fsdp", "cp"),
        P(None, "fsdp", "cp"),
    ) + (P(),) * 7
    return jax.shard_map(steps, mesh=mesh, in_specs=in_specs, out_specs=out_specs, check_vma=False)
```

time: 2680 us -> 733 us (0.27)
  waiting for transfers between devices: 1950 us -> 299 us
  other arithmetic: 223 us -> 42.4 us
  matrix products: 238 us -> 72.5 us
  local copies, waits for them, and re-layouts: 207 us -> 70.2 us
  starting transfers between devices: 13.8 us -> 125 us
  Pallas kernels: 0 us -> 98.2 us
    all_gather x12 -> x4, waiting for transfers between devices: 797 us -> 5.6 us  [gather_cp(): return lax.all_gather(a, 'cp', axis=0)]
    reduce_scatter x6 -> x4, waiting for transfers between devices: 670 us -> 0.05 us  [the longest x2 0.02 us: steps(): d_wo = lax.psum_scatter(d_wo, 'cp', scatter_dimension=0, tiled=True)]
    unnamed x21 -> x8, waiting for transfers between devices: 346 us -> 0.77 us
    ppermute x5 -> x90, waiting for transfers between devices: 0.01 us -> 293 us  [the longest x85 293 us: swap(): return lax.ppermute(a, axis, [(i, i ^ bit) for i in range(size)])]
    dot_general x44 -> x16, matrix products: 238 us -> 72.5 us  [mm(): lax.dot_general(a, b, (((ca,), (cb,)), ((), ())), precision=precision, pr...]
    psum x1 -> x0, waiting for transfers between devices: 135 us -> none  [body(): lax.psum((grad_norm_in, grad_norm_gate, grad_taps, grad_cbias, grad_dtb,...]
    ppermute x5 -> x90, starting transfers between devices: 12.6 us -> 124 us  [the longest x85 115 us: swap(): return lax.ppermute(a, axis, [(i, i ^ bit) for i in range(size)])]
    pallas_call x0 -> x10, Pallas kernels: none -> 98.2 us  [the longest x2 48.3 us: ssd_backward(): pl.pallas_call(functools.partial(bwd_kernel, hp=hp, nh=nh, cps=cps), grid...]
  transfers between devices with their start and end apart: 25 -> 98, of which waited for: 17 -> 47; matrix products, arithmetic and copies ran while one was open for 17% -> 20% of each run, Pallas kernels for 0% -> 10%
where the time goes in v1:
time: 733 us; the launch traced here: 723 us
  waiting for transfers between devices  299 us (41%)
  starting transfers between devices  125 us (17%)
  Pallas kernels  98.2 us (13%)
  matrix products  72.5 us (10%)
  local copies, waits for them, and re-layouts  70.2 us (10%)
  other arithmetic  42.4 us (6%)
  between operations  16.1 us (2%)
    ppermute x85, waiting for transfers between devices, swap(): return lax.ppermute(a, axis, [(i, i ^ bit) for i in range(size)])  293 us
    ppermute x85, starting transfers between devices, swap(): return lax.ppermute(a, axis, [(i, i ^ bit) for i in range(size)])  115 us
    dot_general x16, matrix products, mm(): lax.dot_general(a, b, (((ca,), (cb,)), ((), ())), precision=precision, pr...  72.5 us
    pallas_call x2, Pallas kernels, ssd_backward(): pl.pallas_call(functools.partial(bwd_kernel, hp=hp, nh=nh, cps=cps), grid...  48.3 us
    unnamed x169, local copies, waits for them, and re-layouts  25.2 us
    pallas_call x2, Pallas kernels, ssd_forward(): pl.pallas_call(functools.partial(fwd_kernel, hp=hp, nh=nh, cps=cps), grid...  21.7 us
  transfers between devices with their start and end apart: 98, of which 47 were waited for; matrix products, arithmetic and copies ran while one was open for 20% of the time, Pallas kernels for 10%

profile of v1, /device:TPU:0, one launch (start us, length us, event | category | flops | bytes accessed | tf_op | source)
XLA Modules:
  0.0 723.4 jit_solution(13865583196797675523)
XLA Ops:
  17.2 36.6 %collective-permute-start.1 = (bf16[128,1664]{1,0:T(8,128)(2,1)S(1)}, bf16[128,1664]{1,0:T(8,128)(2,1)S(1)}, u32[]{:S(2)}, u32[]{:S(2)}) collective-permute-start(bf16[128,1664]{1,0:T(8,128)(2,1)S(1)} %collective-permute-done), channel_id=1, source_target_pairs={{0,8},{4,12},{8,0},{12,4},{16,24},{20,28},{24,16},{28,20},{1,9},{5... | collective-permute-start | bytes 1277960 | tf_op jit(solution)/shard_map/ppermute | solution.py:388
  88.5 8.0 %collective-permute-done.9.refs_0_ = bf16[192,1152]{1,0:T(8,128)(2,1)S(1)} collective-permute-done((bf16[192,1152]{1,0:T(8,128)(2,1)S(1)}, bf16[192,1152]{1,0:T(8,128)(2,1)S(1)}, u32[]{:S(2)}, u32[]{:S(2)}) %collective-permute-start.9) | collective-permute-done | bytes 442400 | tf_op jit(solution)/shard_map/ppermute | solution.py:388
  96.5 7.8 %collective-permute-done.10.refs_1_ = bf16[192,1152]{1,0:T(8,128)(2,1)S(1)} collective-permute-done((bf16[192,1152]{1,0:T(8,128)(2,1)S(1)}, bf16[192,1152]{1,0:T(8,128)(2,1)S(1)}, u32[]{:S(2)}, u32[]{:S(2)}) %collective-permute-start.10) | collective-permute-done | bytes 442400 | tf_op jit(solution)/shard_map/ppermute | solution.py:388
  107.7 7.8 %collective-permute-done.11.refs_2_ = bf16[192,1152]{1,0:T(8,128)(2,1)} collective-permute-done((bf16[192,1152]{1,0:T(8,128)(2,1)}, bf16[192,1152]{1,0:T(8,128)(2,1)}, u32[]{:S(2)}, u32[]{:S(2)}) %collective-permute-start.11) | collective-permute-done | bytes 442400 | tf_op jit(solution)/shard_map/ppermute | solution.py:388
  115.5 7.8 %collective-permute-done.13.refs_4_ = bf16[192,1152]{1,0:T(8,128)(2,1)} collective-permute-done((bf16[192,1152]{1,0:T(8,128)(2,1)}, bf16[192,1152]{1,0:T(8,128)(2,1)}, u32[]{:S(2)}, u32[]{:S(2)}) %collective-permute-start.13) | collective-permute-done | bytes 442400 | tf_op jit(solution)/shard_map/ppermute | solution.py:388
  127.9 7.2 fusion.13.p_ref.prev_ref
  137.8 5.8 pack_columns.3.packed
  144.3 10.9 %ssd_forward.2 = (bf16[1024,512]{1,0:T(8,128)(2,1)}, f32[1024,384]{1,0:T(8,128)}, f32[8,128,384]{2,1,0:T(8,128)}) custom-call(s32[1]{0:T(128)} %bitcast.1.f_ref.base_ref, f32[1024,1152]{1,0:T(8,128)} %copy-done, f32[1024,1152]{1,0:T(8,128)} %copy-done, f32[1024,128]{1,0:T(8,128)} %pad.79.meta_ref, f32[8,1024]{1,0:T(8,128)} %broadcast_in_dim.19.seg_ref, ...), custom_call_target="tpu_custom_call" | custom-call | flops 1000000000 | bytes 40000000 | tf_op jit(solution)/shard_map/ssd_forward/pallas_call | solution.py:312
  155.1 5.6 all-gather.9.cloned.1.call-done
  180.0 9.6 %collective-permute-done.17 = bf16[256,768]{1,0:T(8,128)(2,1)S(1)} collective-permute-done((bf16[256,768]{1,0:T(8,128)(2,1)S(1)}, bf16[256,768]{1,0:T(8,128)(2,1)S(1)}, u32[]{:S(2)}, u32[]{:S(2)}) %collective-permute-start.17) | collective-permute-done | bytes 393248 | tf_op jit(solution)/shard_map/ppermute | solution.py:388
  192.1 15.4 %collective-permute-done.19 = bf16[256,896]{1,0:T(8,128)(2,1)S(1)} collective-permute-done((bf16[256,896]{1,0:T(8,128)(2,1)S(1)}, bf16[256,896]{1,0:T(8,128)(2,1)S(1)}, u32[]{:S(2)}, u32[]{:S(2)}) %collective-permute-start.19) | collective-permute-done | bytes 458784 | tf_op jit(solution)/shard_map/ppermute | solution.py:388
  216.2 6.8 collective-permute-done.20
  230.0 6.1 collective-permute-done.27.refs_3_
  238.8 5.8 collective-permute-done.29.refs_5_
  245.9 7.2 collective-permute-done.23
  274.1 8.4 %fusion.112.p_ref.prev_ref = f32[1024,1152]{1,0:T(8,128)} fusion(bf16[1024,1536]{1,0:T(8,128)(2,1)} %constant_dynamic-update-slice_fusion.9, bf16[1536,1152]{1,0:T(8,128)(2,1)S(1)} %bitcast.248), kind=kOutput, calls=%fused_computation.339 | convolution fusion | flops 3623878656 | bytes 11403264 | tf_op jit(solution)/shard_map/dot_general | solution.py:28
  282.4 10.8 %ssd_forward.3 = (bf16[1024,512]{1,0:T(8,128)(2,1)}, f32[1024,384]{1,0:T(8,128)}, f32[8,128,384]{2,1,0:T(8,128)}) custom-call(s32[1]{0:T(128)} %bitcast.1.f_ref.base_ref, f32[1024,1152]{1,0:T(8,128)} %fusion.112.p_ref.prev_ref, f32[1024,1152]{1,0:T(8,128)} %fusion.112.p_ref.prev_ref, f32[1024,128]{1,0:T(8,128)} %pad.79.meta_ref, ...), custom_call_target="tpu_custom_call" | custom-call | flops 1000000000 | bytes 40000000 | tf_op jit(solution)/shard_map/ssd_forward/pallas_call | solution.py:312
  305.0 15.9 %collective-permute-done.38 = bf16[256,768]{1,0:T(8,128)(2,1)S(1)} collective-permute-done((bf16[256,768]{1,0:T(8,128)(2,1)S(1)}, bf16[256,768]{1,0:T(8,128)(2,1)S(1)}, u32[]{:S(2)}, u32[]{:S(2)}) %collective-permute-start.38) | collective-permute-done | bytes 393248 | tf_op jit(solution)/shard_map/ppermute | solution.py:388
  335.3 7.2 collective-permute-done.44
  355.6 24.4 %ssd_backward.2 = (bf16[1024,1152]{1,0:T(8,128)(2,1)}, bf16[1024,384]{1,0:T(8,128)(2,1)}, f32[8,640]{1,0:T(8,128)}, f32[8,384]{1,0:T(8,128)}, f32[8,128]{1,0:T(8,128)}) custom-call(s32[1]{0:T(128)} %bitcast.1.f_ref.base_ref, f32[1024,1152]{1,0:T(8,128)} %fusion.112.p_ref.prev_ref, f32[1024,1152]{1,0:T(8,128)} %fusion.112.p_ref.prev_ref, ...), custom_call_target="tpu_custom_call" | custom-call | flops 1000000000 | bytes 80000000 | tf_op jit(solution)/shard_map/ssd_backward/pallas_call | solution.py:343
  392.1 5.8 convolution_convert_fusion.1
  444.3 7.8 %collective-permute-done.67.refs_3_ = bf16[192,1152]{1,0:T(8,128)(2,1)S(1)} collective-permute-done((bf16[192,1152]{1,0:T(8,128)(2,1)S(1)}, bf16[192,1152]{1,0:T(8,128)(2,1)S(1)}, u32[]{:S(2)}, u32[]{:S(2)}) %collective-permute-start.67) | collective-permute-done | bytes 442400 | tf_op jit(solution)/shard_map/ppermute | solution.py:388
  455.7 21.3 %collective-permute-done.69.refs_5_ = bf16[192,1152]{1,0:T(8,128)(2,1)S(1)} collective-permute-done((bf16[192,1152]{1,0:T(8,128)(2,1)S(1)}, bf16[192,1152]{1,0:T(8,128)(2,1)S(1)}, u32[]{:S(2)}, u32[]{:S(2)}) %collective-permute-start.69) | collective-permute-done | bytes 442400 | tf_op jit(solution)/shard_map/ppermute | solution.py:388
  492.8 24.0 %ssd_backward.3 = (bf16[1024,1152]{1,0:T(8,128)(2,1)}, bf16[1024,384]{1,0:T(8,128)(2,1)}, f32[8,640]{1,0:T(8,128)}, f32[8,384]{1,0:T(8,128)}, f32[8,128]{1,0:T(8,128)}) custom-call(s32[1]{0:T(128)} %bitcast.1.f_ref.base_ref, f32[1024,1152]{1,0:T(8,128)} %copy-done, f32[1024,1152]{1,0:T(8,128)} %copy-done, f32[1024,128]{1,0:T(8,128)} %pad.79.meta_ref, ...), custom_call_target="tpu_custom_call" | custom-call | flops 1000000000 | bytes 80000000 | tf_op jit(solution)/shard_map/ssd_backward/pallas_call | solution.py:343
  524.3 7.6 %convolution_convert_fusion = bf16[1536,1152]{1,0:T(8,128)(2,1)} fusion(bf16[1024,1152]{1,0:T(8,128)(2,1)} %get-tuple-element.178, bf16[1024,1664]{1,0:T(8,128)(2,1)S(1)} %copy-done.46), kind=kOutput, calls=%fused_computation | convolution fusion | flops 3625648128 | bytes 9043968 | tf_op jit(solution)/shard_map/dot_general | solution.py:28
  552.4 6.8 fusion.111
  562.4 6.4 collective-permute-done.77.refs_3_
  572.7 17.6 %collective-permute-done.79.refs_5_ = bf16[192,1152]{1,0:T(8,128)(2,1)} collective-permute-done((bf16[192,1152]{1,0:T(8,128)(2,1)}, bf16[192,1152]{1,0:T(8,128)(2,1)}, u32[]{:S(2)}, u32[]{:S(2)}) %collective-permute-start.79) | collective-permute-done | bytes 442400 | tf_op jit(solution)/shard_map/ppermute | solution.py:388
  590.4 6.6 collective-permute-done.73
  629.0 5.9 collective-permute-done.86
  647.8 50.5 %collective-permute-done.88 = f32[2,8,3328]{2,1,0:T(8,128)S(1)} collective-permute-done((f32[2,8,3328]{2,1,0:T(8,128)S(1)}, f32[2,8,3328]{2,1,0:T(8,128)S(1)}, u32[]{:S(2)}, u32[]{:S(2)}) %collective-permute-start.88) | collective-permute-done | bytes 213024 | tf_op jit(solution)/shard_map/ppermute | solution.py:388
  700.5 9.8 %collective-permute-done.89 = f32[2,8,3328]{2,1,0:T(8,128)S(1)} collective-permute-done((f32[2,8,3328]{2,1,0:T(8,128)S(1)}, f32[2,8,3328]{2,1,0:T(8,128)S(1)}, u32[]{:S(2)}, u32[]{:S(2)}) %collective-permute-start.89) | collective-permute-done | bytes 213024 | tf_op jit(solution)/shard_map/ppermute | solution.py:388
  (569 shorter events, 322.3 us)
Async XLA Ops:
  7.2 66.9 %all-gather.5.cloned.1.call-start = ((), (), s32[]{:S(2)}) async-start(), calls=%async_computation.4 | async-start | bytes 3194880 | tf_op jit(solution)/shard_map/all_gather | solution.py:674
  9.8 128.0 %all-gather.7.cloned.1.call-start = ((), (), s32[]{:S(2)}) async-start(), calls=%async_computation.5 | async-start | bytes 3194880 | tf_op jit(solution)/shard_map/all_gather | solution.py:674
  10.6 150.1 %all-gather.9.cloned.1.call-start = ((), (), s32[]{:S(2)}) async-start(), calls=%async_computation.6 | async-start | bytes 1474560 | tf_op jit(solution)/shard_map/all_gather | solution.py:674
  13.7 279.5 %all-gather.11.cloned.1.call-start = ((), (), s32[]{:S(2)}) async-start(), calls=%async_computation.7 | async-start | bytes 1474560 | tf_op jit(solution)/shard_map/all_gather | solution.py:674
  17.2 44.4 %collective-permute-start.1 = (bf16[128,1664]{1,0:T(8,128)(2,1)S(1)}, bf16[128,1664]{1,0:T(8,128)(2,1)S(1)}, u32[]{:S(2)}, u32[]{:S(2)}) collective-permute-start(bf16[128,1664]{1,0:T(8,128)(2,1)S(1)} %collective-permute-done), channel_id=1, source_target_pairs={{0,8},{4,12},{8,0},{12,4},{16,24},{20,28},{24,16},{28,20},{1,9},{5... | collective-permute-start | bytes 1277960 | tf_op jit(solution)/shard_map/ppermute | solution.py:388
  85.2 30.3 %collective-permute-start.11 = (bf16[192,1152]{1,0:T(8,128)(2,1)}, bf16[192,1152]{1,0:T(8,128)(2,1)}, u32[]{:S(2)}, u32[]{:S(2)}) collective-permute-start(bf16[192,1152]{1,0:T(8,128)(2,1)} %get-tuple-element.248), channel_id=1, source_target_pairs={{0,8},{4,12},{8,0},{12,4},{16,24},{20,28},{24,16},{28,20},{1,9},{5... | collective-permute-start | bytes 1327112 | tf_op jit(solution)/shard_map/ppermute | solution.py:388
  86.7 28.9 %collective-permute-start.12 = (bf16[192,1152]{1,0:T(8,128)(2,1)}, bf16[192,1152]{1,0:T(8,128)(2,1)}, u32[]{:S(2)}, u32[]{:S(2)}) collective-permute-start(bf16[192,1152]{1,0:T(8,128)(2,1)} %get-tuple-element.247), channel_id=1, source_target_pairs={{0,16},{4,20},{8,24},{12,28},{16,0},{20,4},{24,8},{28,12},{1,17},{... | collective-permute-start | bytes 1327112 | tf_op jit(solution)/shard_map/ppermute | solution.py:388
  87.2 36.2 %collective-permute-start.13 = (bf16[192,1152]{1,0:T(8,128)(2,1)}, bf16[192,1152]{1,0:T(8,128)(2,1)}, u32[]{:S(2)}, u32[]{:S(2)}) collective-permute-start(bf16[192,1152]{1,0:T(8,128)(2,1)} %get-tuple-element.246), channel_id=1, source_target_pairs={{0,12},{4,8},{8,4},{12,0},{16,28},{20,24},{24,20},{28,16},{1,13},{... | collective-permute-start | bytes 1327112 | tf_op jit(solution)/shard_map/ppermute | solution.py:388
  96.5 27.6 %collective-permute-start.14 = (bf16[192,1152]{1,0:T(8,128)(2,1)S(1)}, bf16[192,1152]{1,0:T(8,128)(2,1)}, u32[]{:S(2)}, u32[]{:S(2)}) collective-permute-start(bf16[192,1152]{1,0:T(8,128)(2,1)S(1)} %get-tuple-element.245), channel_id=1, source_target_pairs={{0,20},{4,16},{8,28},{12,24},{16,4},{20,0},{24,12},{28,8},{1,21},{... | collective-permute-start | bytes 1327112 | tf_op jit(solution)/shard_map/ppermute | solution.py:388
  166.2 58.5 %collective-permute-start.21 = (bf16[128,1536]{1,0:T(8,128)(2,1)}, bf16[128,1536]{1,0:T(8,128)(2,1)S(1)}, u32[]{:S(2)}, u32[]{:S(2)}) collective-permute-start(bf16[128,1536]{1,0:T(8,128)(2,1)} %get-tuple-element.265), channel_id=1, source_target_pairs={{0,0},{1,4},{2,8},{3,12},{4,3},{5,7},{6,11},{7,15},{8,1},{9,5},{10... | collective-permute-start | bytes 1179656 | tf_op jit(solution)/shard_map/ppermute | solution.py:611
  167.9 349.0 %reduce-scatter.5.cloned.1.call-start = ((), (), s32[]{:S(2)}) async-start(), calls=%async_computation.8 | async-start | bytes 1474560 | tf_op jit(solution)/shard_map/reduce_scatter | solution.py:773
  175.9 31.7 %collective-permute-start.19 = (bf16[256,896]{1,0:T(8,128)(2,1)S(1)}, bf16[256,896]{1,0:T(8,128)(2,1)S(1)}, u32[]{:S(2)}, u32[]{:S(2)}) collective-permute-start(bf16[256,896]{1,0:T(8,128)(2,1)S(1)} %slice.647), channel_id=1, source_target_pairs={{0,16},{4,20},{8,24},{12,28},{16,0},{20,4},{24,8},{28,12},{1,17},{... | collective-permute-start | bytes 1376264 | tf_op jit(solution)/shard_map/ppermute | solution.py:388
  177.7 50.5 %collective-permute-start.24 = (bf16[192,1152]{1,0:T(8,128)(2,1)S(1)}, bf16[192,1152]{1,0:T(8,128)(2,1)S(1)}, u32[]{:S(2)}, u32[]{:S(2)}) collective-permute-start(bf16[192,1152]{1,0:T(8,128)(2,1)S(1)} %get-tuple-element.243), channel_id=1, source_target_pairs={{0,24},{4,28},{8,16},{12,20},{16,8},{20,12},{24,0},{28,4},{1,25},{... | collective-permute-start | bytes 1327112 | tf_op jit(solution)/shard_map/ppermute | solution.py:388
  177.8 51.3 %collective-permute-start.25 = (bf16[192,1152]{1,0:T(8,128)(2,1)S(1)}, bf16[192,1152]{1,0:T(8,128)(2,1)S(1)}, u32[]{:S(2)}, u32[]{:S(2)}) collective-permute-start(bf16[192,1152]{1,0:T(8,128)(2,1)S(1)} %get-tuple-element.242), channel_id=1, source_target_pairs={{0,28},{4,24},{8,20},{12,16},{16,12},{20,8},{24,4},{28,0},{1,29},{... | collective-permute-start | bytes 1327112 | tf_op jit(solution)/shard_map/ppermute | solution.py:388
  189.6 39.4 %collective-permute-start.26 = (bf16[192,1152]{1,0:T(8,128)(2,1)S(1)}, bf16[192,1152]{1,0:T(8,128)(2,1)S(1)}, u32[]{:S(2)}, u32[]{:S(2)}) collective-permute-start(bf16[192,1152]{1,0:T(8,128)(2,1)S(1)} %get-tuple-element.241), channel_id=1, source_target_pairs={{0,8},{4,12},{8,0},{12,4},{16,24},{20,28},{24,16},{28,20},{1,9},{5... | collective-permute-start | bytes 1327112 | tf_op jit(solution)/shard_map/ppermute | solution.py:388
  238.8 29.2 %collective-permute-start.33 = (bf16[128,1536]{1,0:T(8,128)(2,1)}, bf16[128,1536]{1,0:T(8,128)(2,1)}, u32[]{:S(2)}, u32[]{:S(2)}) collective-permute-start(bf16[128,1536]{1,0:T(8,128)(2,1)} %get-tuple-element.218), channel_id=1, source_target_pairs={{0,4},{4,0},{8,12},{12,8},{16,20},{20,16},{24,28},{28,24},{1,5},{5... | collective-permute-start | bytes 1179656 | tf_op jit(solution)/shard_map/ppermute | solution.py:388
  304.3 25.1 %collective-permute-start.43 = (bf16[128,1536]{1,0:T(8,128)(2,1)S(1)}, bf16[128,1536]{1,0:T(8,128)(2,1)S(1)}, u32[]{:S(2)}, u32[]{:S(2)}) collective-permute-start(bf16[128,1536]{1,0:T(8,128)(2,1)S(1)} %convert_element_type.494), channel_id=1, source_target_pairs={{0,0},{1,4},{2,8},{3,12},{4,3},{5,7},{6,11},{7,15},{8,1},{9,5},{10... | collective-permute-start | bytes 1179656 | tf_op jit(solution)/shard_map/ppermute | solution.py:611
  416.7 203.7 %reduce-scatter.7.cloned.1.call-start = ((), (), s32[]{:S(2)}) async-start(), calls=%async_computation.9 | async-start | bytes 3194880 | tf_op jit(solution)/shard_map/reduce_scatter | solution.py:741
  437.4 39.6 %collective-permute-start.69 = (bf16[192,1152]{1,0:T(8,128)(2,1)S(1)}, bf16[192,1152]{1,0:T(8,128)(2,1)S(1)}, u32[]{:S(2)}, u32[]{:S(2)}) collective-permute-start(bf16[192,1152]{1,0:T(8,128)(2,1)S(1)} %get-tuple-element.231), channel_id=1, source_target_pairs={{0,20},{4,16},{8,28},{12,24},{16,4},{20,0},{24,12},{28,8},{1,21},{... | collective-permute-start | bytes 1327112 | tf_op jit(solution)/shard_map/ppermute | solution.py:388
  438.8 38.2 %collective-permute-start.70 = (bf16[192,1152]{1,0:T(8,128)(2,1)S(1)}, bf16[192,1152]{1,0:T(8,128)(2,1)S(1)}, u32[]{:S(2)}, u32[]{:S(2)}) collective-permute-start(bf16[192,1152]{1,0:T(8,128)(2,1)S(1)} %get-tuple-element.230), channel_id=1, source_target_pairs={{0,24},{4,28},{8,16},{12,20},{16,8},{20,12},{24,0},{28,4},{1,25},{... | collective-permute-start | bytes 1327112 | tf_op jit(solution)/shard_map/ppermute | solution.py:388
  444.3 32.7 %collective-permute-start.71 = (bf16[192,1152]{1,0:T(8,128)(2,1)S(1)}, bf16[192,1152]{1,0:T(8,128)(2,1)S(1)}, u32[]{:S(2)}, u32[]{:S(2)}) collective-permute-start(bf16[192,1152]{1,0:T(8,128)(2,1)S(1)} %get-tuple-element.229), channel_id=1, source_target_pairs={{0,28},{4,24},{8,20},{12,16},{16,12},{20,8},{24,4},{28,0},{1,29},{... | collective-permute-start | bytes 1327112 | tf_op jit(solution)/shard_map/ppermute | solution.py:388
  452.1 31.5 %collective-permute-start.63 = (bf16[128,1664]{1,0:T(8,128)(2,1)}, bf16[128,1664]{1,0:T(8,128)(2,1)}, u32[]{:S(2)}, u32[]{:S(2)}) collective-permute-start(bf16[128,1664]{1,0:T(8,128)(2,1)} %pad_maximum_fusion.10), channel_id=1, source_target_pairs={{0,4},{4,0},{8,12},{12,8},{16,20},{20,16},{24,28},{28,24},{1,5},{5... | collective-permute-start | bytes 1277960 | tf_op jit(solution)/shard_map/ppermute | solution.py:388
  454.7 30.7 %collective-permute-start.64 = (bf16[128,1664]{1,0:T(8,128)(2,1)}, bf16[128,1664]{1,0:T(8,128)(2,1)}, u32[]{:S(2)}, u32[]{:S(2)}) collective-permute-start(bf16[128,1664]{1,0:T(8,128)(2,1)} %collective-permute-done.58), channel_id=1, source_target_pairs={{0,4},{4,0},{8,12},{12,8},{16,20},{20,16},{24,28},{28,24},{1,5},{5... | collective-permute-start | bytes 1277960 | tf_op jit(solution)/shard_map/ppermute | solution.py:388
  518.7 126.0 %reduce-scatter.11.cloned.1.call-start = ((), (), s32[]{:S(2)}) async-start(), calls=%async_computation.11 | async-start | bytes 1474560 | tf_op jit(solution)/shard_map/reduce_scatter | solution.py:773
  551.2 162.4 %reduce-scatter.9.cloned.1.call-start = ((), (), s32[]{:S(2)}) async-start(), calls=%async_computation.10 | async-start | bytes 3194880 | tf_op jit(solution)/shard_map/reduce_scatter | solution.py:741
  551.2 39.1 %collective-permute-start.79 = (bf16[192,1152]{1,0:T(8,128)(2,1)}, bf16[192,1152]{1,0:T(8,128)(2,1)}, u32[]{:S(2)}, u32[]{:S(2)}) collective-permute-start(bf16[192,1152]{1,0:T(8,128)(2,1)} %get-tuple-element.223), channel_id=1, source_target_pairs={{0,20},{4,16},{8,28},{12,24},{16,4},{20,0},{24,12},{28,8},{1,21},{... | collective-permute-start | bytes 1327112 | tf_op jit(solution)/shard_map/ppermute | solution.py:388
  560.1 30.2 %collective-permute-start.80 = (bf16[192,1152]{1,0:T(8,128)(2,1)}, bf16[192,1152]{1,0:T(8,128)(2,1)}, u32[]{:S(2)}, u32[]{:S(2)}) collective-permute-start(bf16[192,1152]{1,0:T(8,128)(2,1)} %get-tuple-element.222), channel_id=1, source_target_pairs={{0,24},{4,28},{8,16},{12,20},{16,8},{20,12},{24,0},{28,4},{1,25},{... | collective-permute-start | bytes 1327112 | tf_op jit(solution)/shard_map/ppermute | solution.py:388
  561.7 28.7 %collective-permute-start.81 = (bf16[192,1152]{1,0:T(8,128)(2,1)}, bf16[192,1152]{1,0:T(8,128)(2,1)}, u32[]{:S(2)}, u32[]{:S(2)}) collective-permute-start(bf16[192,1152]{1,0:T(8,128)(2,1)} %get-tuple-element.221), channel_id=1, source_target_pairs={{0,28},{4,24},{8,20},{12,16},{16,12},{20,8},{24,4},{28,0},{1,29},{... | collective-permute-start | bytes 1327112 | tf_op jit(solution)/shard_map/ppermute | solution.py:388
  568.8 28.2 %collective-permute-start.73 = (bf16[256,768]{1,0:T(8,128)(2,1)}, bf16[256,768]{1,0:T(8,128)(2,1)}, u32[]{:S(2)}, u32[]{:S(2)}) collective-permute-start(bf16[256,768]{1,0:T(8,128)(2,1)} %get-tuple-element.258), channel_id=1, source_target_pairs={{0,8},{4,12},{8,0},{12,4},{16,24},{20,28},{24,16},{28,20},{1,9},{5... | collective-permute-start | bytes 1179656 | tf_op jit(solution)/shard_map/ppermute | solution.py:388
  570.0 29.0 %collective-permute-start.74 = (bf16[256,768]{1,0:T(8,128)(2,1)}, bf16[256,768]{1,0:T(8,128)(2,1)}, u32[]{:S(2)}, u32[]{:S(2)}) collective-permute-start(bf16[256,768]{1,0:T(8,128)(2,1)} %get-tuple-element.257), channel_id=1, source_target_pairs={{0,16},{4,20},{8,24},{12,28},{16,0},{20,4},{24,8},{28,12},{1,17},{... | collective-permute-start | bytes 1179656 | tf_op jit(solution)/shard_map/ppermute | solution.py:388
  638.7 59.8 %collective-permute-start.84 = (bf16[128,1536]{1,0:T(8,128)(2,1)}, bf16[128,1536]{1,0:T(8,128)(2,1)}, u32[]{:S(2)}, u32[]{:S(2)}) collective-permute-start(bf16[128,1536]{1,0:T(8,128)(2,1)} %add_convert_fusion), channel_id=1, source_target_pairs={{0,0},{4,1},{8,2},{12,3},{3,4},{7,5},{11,6},{15,7},{1,8},{5,9},{9,... | collective-permute-start | bytes 1179656 | tf_op jit(solution)/shard_map/ppermute | solution.py:611
  643.3 55.1 %collective-permute-start.88 = (f32[2,8,3328]{2,1,0:T(8,128)S(1)}, f32[2,8,3328]{2,1,0:T(8,128)S(1)}, u32[]{:S(2)}, u32[]{:S(2)}) collective-permute-start(f32[2,8,3328]{2,1,0:T(8,128)S(1)} %add.467), channel_id=1, source_target_pairs={{0,1},{1,0},{2,3},{3,2},{4,5},{5,4},{6,7},{7,6},{8,9},{9,8},{10,11... | collective-permute-start | bytes 638984 | tf_op jit(solution)/shard_map/ppermute | solution.py:388
  (130 other events, 1653.3 us)
Sparse Core Ops, SparseCore 0:
  10.2 63.4 all-gather.4
  75.8 54.1 all-gather.6
  131.6 29.0 all-gather.8
  168.0 36.0 all-gather.10
  416.8 26.5 reduce-scatter.4
  518.8 48.4 reduce-scatter.6
  570.2 28.8 reduce-scatter.10
  622.8 76.9 reduce-scatter.8

commit v2 on v1

--- a/solution.py
+++ b/solution.py
@@ -392,12 +392,11 @@
     return (6, 7, 2, 4, 3, 5, 1) if count == 8 else tuple(range(1, count))
 
 
-def sum_all(a):
-    for axis in ("fsdp", "cp"):
-        bit = 1
-        while bit < lax.axis_size(axis):
-            a = a + swap(a, axis, bit)
-            bit *= 2
+def sum_over(axis, a):
+    bit = 1
+    while bit < lax.axis_size(axis):
+        a = a + swap(a, axis, bit)
+        bit *= 2
     return a
 
 
@@ -425,7 +424,7 @@
     return jnp.concatenate(parts, axis=0), beside
 
 
-def scatter_plane(rows, weight, contract, split, beside=(None, None)):
+def scatter_plane(rows, weight, contract, split, beside=(None, None), hold=()):
     fs = lax.axis_size("fsdp")
     half = rows.shape[0] // 2
     one, two = beside
@@ -434,6 +433,8 @@
     if one is not None:
         mate, one = together(mate, one)
     total = mm(rows[:half], weight, 1, contract) + mate.astype(F32)
+    if hold:
+        total, *hold = together(total, *hold)
     if fs != 8:
         bit = fs // 2
         while bit > 1:
@@ -441,7 +442,7 @@
             got = swap(total[half:].astype(BF16), "fsdp", bit)
             total = total[:half] + got.astype(F32)
             bit //= 2
-        return total, one, two
+        return total, one, two, hold
     g = GROUP
     sent_x = swap(total[g : 3 * g, :split].astype(BF16), "fsdp", 2)
     sent_y = swap(total[2 * g :, split:].astype(BF16), "fsdp", 4)
@@ -453,7 +454,7 @@
     last_x = swap(turn_x, "fsdp", 2)
     left = total[:g, :split] + sent_x[:g].astype(F32) + last_y.astype(F32)
     right = total[:g, split:] + sent_y[g:].astype(F32) + last_x.astype(F32)
-    return jnp.concatenate([left, right], axis=1), one, two
+    return jnp.concatenate([left, right], axis=1), one, two, hold
 
 
 def column_pieces(fs, cp):
@@ -624,7 +625,6 @@
         jnp.concatenate([seg_ids.reshape(GROUP, 1).astype(BF16), high, low], axis=1), 1, LANES
     )
     moved = move(jnp.concatenate([normed, marks], axis=1), there)
-    left_over = move(left_over, there)
     own_scale = moved[:, width + 1 : width + 3]
     own_normed = moved[:, :width]
     marked, _ = gather_plane(moved)
@@ -676,7 +676,9 @@
     got_in, got_out = [None] * LAYERS, [None] * LAYERS
     got_in[0] = gather_cp(w_in[0])
     last_grad = d_out.reshape(GROUP, width)
+    got_in[0], left_over = together(got_in[0], left_over)
     packed = pack(jnp.zeros((1,), F32), got_in[0], wid, fs, cp)
+    left_over = move(left_over, there)
     full_in, full_out = [place_in(packed, send_in(packed))], []
     for i in range(LAYERS):
         if i:
@@ -715,7 +717,7 @@
         rg, y, states = ssd_forward(base, project, meta, seg_rows, *params[i], **sizes)
         rg, got_out[i] = together(rg, got_out[i])
         full_out.append(finish_out(got_out[i]))
-        summed, _, _ = scatter_plane(rg, full_out[i], 0, width // 2)
+        summed, *_ = scatter_plane(rg, full_out[i], 0, width // 2)
         inv = lax.rsqrt(
             jnp.sum(summed[:, width:], axis=1, keepdims=True) * (1.0 / INNER) + EPSILON
         )
@@ -728,6 +730,7 @@
     activations = first + move(added.astype(BF16), back).astype(F32)
 
     grads_in, grads_out, small = [None] * LAYERS, [None] * LAYERS, [None] * LAYERS
+    norm_sums = {}
     change = 0.0
     waiting = None
 
@@ -756,19 +759,28 @@
         gp, gated, gcw, gch, gdt = ssd_backward(
             base, project, meta, seg_rows, *params[i], y, states, gx, **sizes
         )
+        rate = -jnp.exp(own(a_log[i], heads, heads))
+        by_head = jnp.sum(gch[0, :hc].reshape(heads, HEADDIM), axis=1)
+        thin = jnp.concatenate([gdt[0, :heads], gdt[1, :heads] * rate, by_head])
+        rows = [gcw[:5], gch[1:2], thin[None]]
+        rows += [norm_sums[i + 1][None]] if i + 1 < LAYERS else [thin[None]]
+        small[i] = jnp.concatenate([pad_to(row, 1, width) for row in rows], axis=0)
         if waiting is not None:
-            gp, wide, grads_out[i + 1] = together(gp, wide, grads_out[i + 1])
+            tables = sum_over("cp", jnp.stack(small))
+            gp, wide, grads_out[i + 1], tables = together(gp, wide, grads_out[i + 1], tables)
             grads_in[i + 1] = sum_in(wide)
         d_wi = mm(normed_all, gp, 0, 0).astype(BF16).reshape(fs, rows_in, wid)
         d_wo = mm(gated[:, :hc], payload[:, :width], 0, 0).astype(BF16)
         if i:
-            g_normed, d_wo, waiting = scatter_plane(
+            g_normed, d_wo, waiting, _ = scatter_plane(
                 gp, full_in[i], 1, width // 2, (d_wo, [d_wi])
             )
         else:
             gp, d_wi, d_wo = together(gp, d_wi, d_wo)
             blocks = send_out(d_wi)
-            g_normed, _, blocks = scatter_plane(gp, full_in[i], 1, width // 2, (None, blocks))
+            g_normed, tables, blocks, _ = scatter_plane(
+                gp, full_in[i], 1, width // 2, (tables, blocks)
+            )
         d_wo = d_wo.reshape(hc, cp, width // cp).transpose(1, 0, 2)
         d_wo = lax.psum_scatter(d_wo, "cp", scatter_dimension=0, tiled=True)
         grads_out[i] = d_wo[0].astype(F32)
@@ -781,30 +793,27 @@
         hat = before * scale
         pulled = g_normed * norm_in[i]
         change = change + scale * (pulled - hat * jnp.mean(pulled * hat, axis=-1, keepdims=True))
-        g_norm_in = jnp.sum(g_normed * hat, axis=0)
-
-        table = jnp.zeros((8, CHANNELS), F32)
-        mine = jnp.concatenate([gcw[:5, :hc], gch[1:2, :hc]], axis=0)
-        table = lax.dynamic_update_slice(table, mine, (0, f * hc))
-        table = table.at[:5, INNER:].add(gcw[:5, hp:])
-        table = table.at[6, :width].set(g_norm_in)
-        by_head = jnp.sum(gch[0, :hc].reshape(heads, HEADDIM), axis=1)
-        rate = -jnp.exp(own(a_log[i], heads, heads))
-        thin = jnp.stack([gdt[0, :heads], gdt[1, :heads] * rate, by_head])
-        thin = lax.dynamic_update_slice(jnp.zeros((3, HEADS), F32), thin, (0, f * heads))
-        table = table.at[7, : 3 * HEADS].set(thin.reshape(-1))
-        small[i] = table
+        norm_sums[i] = jnp.sum(g_normed * hat, axis=0)
 
     d_hidden = last_grad + move(change.astype(BF16), back).astype(F32)
-    tables = sum_all(jnp.stack(small))
     shape = hidden.shape
-    thin = tables[:, 7, : 3 * HEADS].reshape(LAYERS, 3, HEADS)
+    first_norm = jnp.broadcast_to(norm_sums[0].reshape(1, -1, LANES), (1, width // LANES, LANES))
+    first_norm = sum_over("cp", sum_over("fsdp", first_norm)).reshape(1, width)
+    full = jnp.zeros((LAYERS, 8, CHANNELS), F32)
+    full = lax.dynamic_update_slice(full, tables[:, :6, :hc], (0, 0, f * hc))
+    full = full.at[:, :5, INNER:].set(tables[:, :5, hp : hp + 2 * STATE])
+    thin = tables[:, 6, : 3 * heads].reshape(LAYERS, 3, heads)
+    thin = lax.dynamic_update_slice(jnp.zeros((LAYERS, 3, HEADS), F32), thin, (0, 0, f * heads))
+    full = full.at[:, 6, : 3 * HEADS].set(thin.reshape(LAYERS, 3 * HEADS))
+    full = full.at[:-1, 7, :width].set(tables[:-1, 7])
+    tables = sum_over("fsdp", full)
+    thin = tables[:, 6, : 3 * HEADS].reshape(LAYERS, 3, HEADS)
     return (
         activations.reshape(shape),
         d_hidden.reshape(shape),
         jnp.stack(grads_in),
         jnp.stack(grads_out),
-        tables[:, 6, :width],
+        jnp.concatenate([first_norm, tables[:-1, 7, :width]], axis=0),
         tables[:, 5, :INNER],
         tables[:, :4],
         tables[:, 4],

time: 733 us -> 706 us (0.963)
  waiting for transfers between devices: 299 us -> 263 us
  starting transfers between devices: 125 us -> 145 us
  local copies, waits for them, and re-layouts: 70.2 us -> 59.3 us
    ppermute x85 -> x90, waiting for transfers between devices: 293 us -> 257 us  [swap(): return lax.ppermute(a, axis, [(i, i ^ bit) for i in range(size)])]
    ppermute x85 -> x90, starting transfers between devices: 115 us -> 136 us  [swap(): return lax.ppermute(a, axis, [(i, i ^ bit) for i in range(size)])]
    unnamed x169 -> x177, local copies, waits for them, and re-layouts: 25.2 us -> 15.6 us
  transfers between devices with their start and end apart: 98 -> 103, of which waited for: 47 -> 55; matrix products, arithmetic and copies ran while one was open for 20% -> 19% of each run, Pallas kernels for 10% -> 11%
where the time goes in v2:
time: 706 us; the launch traced here: 696 us
  waiting for transfers between devices  263 us (37%)
  starting transfers between devices  145 us (21%)
  Pallas kernels  98.1 us (14%)
  matrix products  72.1 us (10%)
  local copies, waits for them, and re-layouts  59.3 us (8%)
  other arithmetic  41 us (6%)
  between operations  16.2 us (2%)
    ppermute x90, waiting for transfers between devices, swap(): return lax.ppermute(a, axis, [(i, i ^ bit) for i in range(size)])  257 us
    ppermute x90, starting transfers between devices, swap(): return lax.ppermute(a, axis, [(i, i ^ bit) for i in range(size)])  136 us
    dot_general x16, matrix products, mm(): lax.dot_general(a, b, (((ca,), (cb,)), ((), ())), precision=precision, pr...  72.1 us
    pallas_call x2, Pallas kernels, ssd_backward(): pl.pallas_call(functools.partial(bwd_kernel, hp=hp, nh=nh, cps=cps), grid...  48.1 us
    pallas_call x2, Pallas kernels, ssd_forward(): pl.pallas_call(functools.partial(fwd_kernel, hp=hp, nh=nh, cps=cps), grid...  21.6 us
    unnamed x177, local copies, waits for them, and re-layouts  15.6 us
  transfers between devices with their start and end apart: 103, of which 55 were waited for; matrix products, arithmetic and copies ran while one was open for 19% of the time, Pallas kernels for 11%

profile of v2, /device:TPU:0, one launch (start us, length us, event | category | flops | bytes accessed | tf_op | source)
XLA Modules:
  0.0 695.6 jit_solution(11975066271428466848)
XLA Ops:
  17.2 36.6 %collective-permute-start.1 = (bf16[128,1664]{1,0:T(8,128)(2,1)S(1)}, bf16[128,1664]{1,0:T(8,128)(2,1)S(1)}, u32[]{:S(2)}, u32[]{:S(2)}) collective-permute-start(bf16[128,1664]{1,0:T(8,128)(2,1)S(1)} %collective-permute-done), channel_id=1, source_target_pairs={{0,8},{4,12},{8,0},{12,4},{16,24},{20,28},{24,16},{28,20},{1,9},{5... | collective-permute-start | bytes 1277960 | tf_op jit(solution)/shard_map/ppermute | solution.py:388
  56.0 5.5 collective-permute-done.1
  88.5 8.0 %collective-permute-done.9.refs_0_ = bf16[192,1152]{1,0:T(8,128)(2,1)S(1)} collective-permute-done((bf16[192,1152]{1,0:T(8,128)(2,1)S(1)}, bf16[192,1152]{1,0:T(8,128)(2,1)S(1)}, u32[]{:S(2)}, u32[]{:S(2)}) %collective-permute-start.9) | collective-permute-done | bytes 442400 | tf_op jit(solution)/shard_map/ppermute | solution.py:388
  96.5 7.8 %collective-permute-done.10.refs_1_ = bf16[192,1152]{1,0:T(8,128)(2,1)S(1)} collective-permute-done((bf16[192,1152]{1,0:T(8,128)(2,1)S(1)}, bf16[192,1152]{1,0:T(8,128)(2,1)S(1)}, u32[]{:S(2)}, u32[]{:S(2)}) %collective-permute-start.10) | collective-permute-done | bytes 442400 | tf_op jit(solution)/shard_map/ppermute | solution.py:388
  107.8 7.8 %collective-permute-done.11.refs_2_ = bf16[192,1152]{1,0:T(8,128)(2,1)} collective-permute-done((bf16[192,1152]{1,0:T(8,128)(2,1)}, bf16[192,1152]{1,0:T(8,128)(2,1)}, u32[]{:S(2)}, u32[]{:S(2)}) %collective-permute-start.11) | collective-permute-done | bytes 442400 | tf_op jit(solution)/shard_map/ppermute | solution.py:388
  115.6 7.8 %collective-permute-done.13.refs_4_ = bf16[192,1152]{1,0:T(8,128)(2,1)} collective-permute-done((bf16[192,1152]{1,0:T(8,128)(2,1)}, bf16[192,1152]{1,0:T(8,128)(2,1)}, u32[]{:S(2)}, u32[]{:S(2)}) %collective-permute-start.13) | collective-permute-done | bytes 442400 | tf_op jit(solution)/shard_map/ppermute | solution.py:388
  127.9 7.2 %fusion.13.p_ref.prev_ref = f32[1024,1152]{1,0:T(8,128)S(1)} fusion(bf16[1536,1152]{1,0:T(8,128)(2,1)} %bitcast.262, bf16[1024,1664]{1,0:T(8,128)(2,1)} %copy-done.40), kind=kOutput, calls=%fused_computation.20 | convolution fusion | flops 3623878656 | bytes 11403264 | tf_op jit(solution)/shard_map/dot_general | solution.py:28
  137.8 5.9 pack_columns.3.packed
  144.3 10.8 %ssd_forward.2 = (bf16[1024,512]{1,0:T(8,128)(2,1)}, f32[1024,384]{1,0:T(8,128)}, f32[8,128,384]{2,1,0:T(8,128)}) custom-call(s32[1]{0:T(128)} %bitcast.1.f_ref.base_ref, f32[1024,1152]{1,0:T(8,128)} %copy-done, f32[1024,1152]{1,0:T(8,128)} %copy-done, f32[1024,128]{1,0:T(8,128)} %pad.93.meta_ref, f32[8,1024]{1,0:T(8,128)} %broadcast_in_dim.29.seg_ref, ...), custom_call_target="tpu_custom_call" | custom-call | flops 1000000000 | bytes 40000000 | tf_op jit(solution)/shard_map/ssd_forward/pallas_call | solution.py:312
  155.1 5.5 all-gather.9.cloned.1.call-done
  189.5 16.6 %collective-permute-done.19 = bf16[256,896]{1,0:T(8,128)(2,1)S(1)} collective-permute-done((bf16[256,896]{1,0:T(8,128)(2,1)S(1)}, bf16[256,896]{1,0:T(8,128)(2,1)S(1)}, u32[]{:S(2)}, u32[]{:S(2)}) %collective-permute-start.19) | collective-permute-done | bytes 458784 | tf_op jit(solution)/shard_map/ppermute | solution.py:388
  216.6 8.5 %collective-permute-done.20 = bf16[128,896]{1,0:T(8,128)(2,1)S(1)} collective-permute-done((bf16[128,896]{1,0:T(8,128)(2,1)S(1)}, bf16[128,896]{1,0:T(8,128)(2,1)S(1)}, u32[]{:S(2)}, u32[]{:S(2)}) %collective-permute-start.20) | collective-permute-done | bytes 229408 | tf_op jit(solution)/shard_map/ppermute | solution.py:388
  232.6 5.5 collective-permute-done.27.refs_3_
  240.8 5.8 collective-permute-done.29.refs_5_
  247.7 6.6 collective-permute-done.23
  273.2 8.4 %fusion.118.p_ref.prev_ref = f32[1024,1152]{1,0:T(8,128)} fusion(bf16[1024,1536]{1,0:T(8,128)(2,1)} %constant_dynamic-update-slice_fusion.9, bf16[1536,1152]{1,0:T(8,128)(2,1)S(1)} %bitcast.266), kind=kOutput, calls=%fused_computation.359 | convolution fusion | flops 3623878656 | bytes 11403264 | tf_op jit(solution)/shard_map/dot_general | solution.py:28
  281.5 10.8 %ssd_forward.3 = (bf16[1024,512]{1,0:T(8,128)(2,1)}, f32[1024,384]{1,0:T(8,128)}, f32[8,128,384]{2,1,0:T(8,128)}) custom-call(s32[1]{0:T(128)} %bitcast.1.f_ref.base_ref, f32[1024,1152]{1,0:T(8,128)} %fusion.118.p_ref.prev_ref, f32[1024,1152]{1,0:T(8,128)} %fusion.118.p_ref.prev_ref, f32[1024,128]{1,0:T(8,128)} %pad.93.meta_ref, ...), custom_call_target="tpu_custom_call" | custom-call | flops 1000000000 | bytes 40000000 | tf_op jit(solution)/shard_map/ssd_forward/pallas_call | solution.py:312
  304.8 15.9 %collective-permute-done.38 = bf16[256,768]{1,0:T(8,128)(2,1)S(1)} collective-permute-done((bf16[256,768]{1,0:T(8,128)(2,1)S(1)}, bf16[256,768]{1,0:T(8,128)(2,1)S(1)}, u32[]{:S(2)}, u32[]{:S(2)}) %collective-permute-start.38) | collective-permute-done | bytes 393248 | tf_op jit(solution)/shard_map/ppermute | solution.py:388
  335.0 7.2 %collective-permute-done.44 = bf16[128,1664]{1,0:T(8,128)(2,1)S(1)} collective-permute-done((bf16[128,1664]{1,0:T(8,128)(2,1)S(1)}, bf16[128,1664]{1,0:T(8,128)(2,1)S(1)}, u32[]{:S(2)}, u32[]{:S(2)}) %collective-permute-start.44) | collective-permute-done | bytes 426016 | tf_op jit(solution)/shard_map/ppermute | solution.py:388
  355.4 24.2 %ssd_backward.2 = (bf16[1024,1152]{1,0:T(8,128)(2,1)}, bf16[1024,384]{1,0:T(8,128)(2,1)}, f32[8,640]{1,0:T(8,128)}, f32[8,384]{1,0:T(8,128)}, f32[8,128]{1,0:T(8,128)}) custom-call(s32[1]{0:T(128)} %bitcast.1.f_ref.base_ref, f32[1024,1152]{1,0:T(8,128)} %fusion.118.p_ref.prev_ref, f32[1024,1152]{1,0:T(8,128)} %fusion.118.p_ref.prev_ref, ...), custom_call_target="tpu_custom_call" | custom-call | flops 1000000000 | bytes 80000000 | tf_op jit(solution)/shard_map/ssd_backward/pallas_call | solution.py:343
  379.6 5.9 convolution_convert_fusion.3
  397.6 5.8 convolution_convert_fusion.1
  444.6 24.0 %ssd_backward.3 = (bf16[1024,1152]{1,0:T(8,128)(2,1)}, bf16[1024,384]{1,0:T(8,128)(2,1)}, f32[8,640]{1,0:T(8,128)}, f32[8,384]{1,0:T(8,128)}, f32[8,128]{1,0:T(8,128)}) custom-call(s32[1]{0:T(128)} %bitcast.1.f_ref.base_ref, f32[1024,1152]{1,0:T(8,128)} %copy-done, f32[1024,1152]{1,0:T(8,128)} %copy-done, f32[1024,128]{1,0:T(8,128)} %pad.93.meta_ref, ...), custom_call_target="tpu_custom_call" | custom-call | flops 1000000000 | bytes 80000000 | tf_op jit(solution)/shard_map/ssd_backward/pallas_call | solution.py:343
  477.5 6.8 collective-permute-done.67.refs_3_
  485.4 19.5 %collective-permute-done.68.refs_4_ = bf16[192,1152]{1,0:T(8,128)(2,1)} collective-permute-done((bf16[192,1152]{1,0:T(8,128)(2,1)}, bf16[192,1152]{1,0:T(8,128)(2,1)}, u32[]{:S(2)}, u32[]{:S(2)}) %collective-permute-start.68) | collective-permute-done | bytes 442400 | tf_op jit(solution)/shard_map/ppermute | solution.py:388
  504.9 8.2 %collective-permute-done.69.refs_5_ = bf16[192,1152]{1,0:T(8,128)(2,1)} collective-permute-done((bf16[192,1152]{1,0:T(8,128)(2,1)}, bf16[192,1152]{1,0:T(8,128)(2,1)}, u32[]{:S(2)}, u32[]{:S(2)}) %collective-permute-start.69) | collective-permute-done | bytes 442400 | tf_op jit(solution)/shard_map/ppermute | solution.py:388
  523.7 7.6 %convolution_convert_fusion = bf16[1536,1152]{1,0:T(8,128)(2,1)} fusion(bf16[1024,1152]{1,0:T(8,128)(2,1)} %get-tuple-element.155, bf16[1024,1664]{1,0:T(8,128)(2,1)S(1)} %copy-done.41), kind=kOutput, calls=%fused_computation | convolution fusion | flops 3625648128 | bytes 9043968 | tf_op jit(solution)/shard_map/dot_general | solution.py:28
  543.6 5.4 fusion.117
  553.6 8.0 %collective-permute-done.79.refs_3_ = bf16[192,1152]{1,0:T(8,128)(2,1)} collective-permute-done((bf16[192,1152]{1,0:T(8,128)(2,1)S(1)}, bf16[192,1152]{1,0:T(8,128)(2,1)}, u32[]{:S(2)}, u32[]{:S(2)}) %collective-permute-start.79) | collective-permute-done | bytes 442400 | tf_op jit(solution)/shard_map/ppermute | solution.py:388
  573.9 8.6 %collective-permute-done.81.refs_5_ = bf16[192,1152]{1,0:T(8,128)(2,1)} collective-permute-done((bf16[192,1152]{1,0:T(8,128)(2,1)}, bf16[192,1152]{1,0:T(8,128)(2,1)}, u32[]{:S(2)}, u32[]{:S(2)}) %collective-permute-start.81) | collective-permute-done | bytes 442400 | tf_op jit(solution)/shard_map/ppermute | solution.py:388
  621.2 8.0 %collective-permute-start.87 = (f32[1,12,128]{2,1,0:T(8,128)S(1)}, f32[1,12,128]{2,1,0:T(8,128)S(1)}, u32[]{:S(2)}, u32[]{:S(2)}) collective-permute-start(f32[1,12,128]{2,1,0:T(8,128)S(1)} %bitcast.283), channel_id=1, source_target_pairs={{0,4},{4,0},{8,12},{12,8},{16,20},{20,16},{24,28},{28,24},{1,5},{5... | collective-permute-start | bytes 18440 | tf_op jit(solution)/shard_map/ppermute | solution.py:388
  648.3 34.7 %collective-permute-done.91 = f32[1,12,128]{2,1,0:T(8,128)S(1)} collective-permute-done((f32[1,12,128]{2,1,0:T(8,128)S(1)}, f32[1,12,128]{2,1,0:T(8,128)S(1)}, u32[]{:S(2)}, u32[]{:S(2)}) %collective-permute-start.91) | collective-permute-done | bytes 6176 | tf_op jit(solution)/shard_map/ppermute | solution.py:388
  (588 shorter events, 324.3 us)
Async XLA Ops:
  7.2 67.0 %all-gather.5.cloned.1.call-start = ((), (), s32[]{:S(2)}) async-start(), calls=%async_computation.4 | async-start | bytes 3194880 | tf_op jit(solution)/shard_map/all_gather | solution.py:674
  9.8 128.0 %all-gather.7.cloned.1.call-start = ((), (), s32[]{:S(2)}) async-start(), calls=%async_computation.5 | async-start | bytes 3194880 | tf_op jit(solution)/shard_map/all_gather | solution.py:674
  10.6 150.1 %all-gather.9.cloned.1.call-start = ((), (), s32[]{:S(2)}) async-start(), calls=%async_computation.6 | async-start | bytes 1474560 | tf_op jit(solution)/shard_map/all_gather | solution.py:674
  13.7 278.7 %all-gather.11.cloned.1.call-start = ((), (), s32[]{:S(2)}) async-start(), calls=%async_computation.7 | async-start | bytes 1474560 | tf_op jit(solution)/shard_map/all_gather | solution.py:674
  17.2 44.4 %collective-permute-start.1 = (bf16[128,1664]{1,0:T(8,128)(2,1)S(1)}, bf16[128,1664]{1,0:T(8,128)(2,1)S(1)}, u32[]{:S(2)}, u32[]{:S(2)}) collective-permute-start(bf16[128,1664]{1,0:T(8,128)(2,1)S(1)} %collective-permute-done), channel_id=1, source_target_pairs={{0,8},{4,12},{8,0},{12,4},{16,24},{20,28},{24,16},{28,20},{1,9},{5... | collective-permute-start | bytes 1277960 | tf_op jit(solution)/shard_map/ppermute | solution.py:388
  85.2 30.3 %collective-permute-start.11 = (bf16[192,1152]{1,0:T(8,128)(2,1)}, bf16[192,1152]{1,0:T(8,128)(2,1)}, u32[]{:S(2)}, u32[]{:S(2)}) collective-permute-start(bf16[192,1152]{1,0:T(8,128)(2,1)} %get-tuple-element.222), channel_id=1, source_target_pairs={{0,8},{4,12},{8,0},{12,4},{16,24},{20,28},{24,16},{28,20},{1,9},{5... | collective-permute-start | bytes 1327112 | tf_op jit(solution)/shard_map/ppermute | solution.py:388
  86.7 28.9 %collective-permute-start.12 = (bf16[192,1152]{1,0:T(8,128)(2,1)}, bf16[192,1152]{1,0:T(8,128)(2,1)}, u32[]{:S(2)}, u32[]{:S(2)}) collective-permute-start(bf16[192,1152]{1,0:T(8,128)(2,1)} %get-tuple-element.221), channel_id=1, source_target_pairs={{0,16},{4,20},{8,24},{12,28},{16,0},{20,4},{24,8},{28,12},{1,17},{... | collective-permute-start | bytes 1327112 | tf_op jit(solution)/shard_map/ppermute | solution.py:388
  87.2 36.2 %collective-permute-start.13 = (bf16[192,1152]{1,0:T(8,128)(2,1)}, bf16[192,1152]{1,0:T(8,128)(2,1)}, u32[]{:S(2)}, u32[]{:S(2)}) collective-permute-start(bf16[192,1152]{1,0:T(8,128)(2,1)} %get-tuple-element.220), channel_id=1, source_target_pairs={{0,12},{4,8},{8,4},{12,0},{16,28},{20,24},{24,20},{28,16},{1,13},{... | collective-permute-start | bytes 1327112 | tf_op jit(solution)/shard_map/ppermute | solution.py:388
  96.5 27.6 %collective-permute-start.14 = (bf16[192,1152]{1,0:T(8,128)(2,1)S(1)}, bf16[192,1152]{1,0:T(8,128)(2,1)}, u32[]{:S(2)}, u32[]{:S(2)}) collective-permute-start(bf16[192,1152]{1,0:T(8,128)(2,1)S(1)} %get-tuple-element.219), channel_id=1, source_target_pairs={{0,20},{4,16},{8,28},{12,24},{16,4},{20,0},{24,12},{28,8},{1,21},{... | collective-permute-start | bytes 1327112 | tf_op jit(solution)/shard_map/ppermute | solution.py:388
  166.2 351.8 %reduce-scatter.5.cloned.1.call-start = ((), (), s32[]{:S(2)}) async-start(), calls=%async_computation.8 | async-start | bytes 1474560 | tf_op jit(solution)/shard_map/reduce_scatter | solution.py:785
  174.8 51.9 %collective-permute-start.21 = (bf16[128,1536]{1,0:T(8,128)(2,1)S(1)}, bf16[128,1536]{1,0:T(8,128)(2,1)S(1)}, u32[]{:S(2)}, u32[]{:S(2)}) collective-permute-start(bf16[128,1536]{1,0:T(8,128)(2,1)S(1)} %copy-done.39), channel_id=1, source_target_pairs={{0,0},{1,4},{2,8},{3,12},{4,3},{5,7},{6,11},{7,15},{8,1},{9,5},{10... | collective-permute-start | bytes 1179656 | tf_op jit(solution)/shard_map/ppermute | solution.py:612
  175.7 30.4 %collective-permute-start.19 = (bf16[256,896]{1,0:T(8,128)(2,1)S(1)}, bf16[256,896]{1,0:T(8,128)(2,1)S(1)}, u32[]{:S(2)}, u32[]{:S(2)}) collective-permute-start(bf16[256,896]{1,0:T(8,128)(2,1)S(1)} %slice.623), channel_id=1, source_target_pairs={{0,16},{4,20},{8,24},{12,28},{16,0},{20,4},{24,8},{28,12},{1,17},{... | collective-permute-start | bytes 1376264 | tf_op jit(solution)/shard_map/ppermute | solution.py:388
  177.5 52.4 %collective-permute-start.24 = (bf16[192,1152]{1,0:T(8,128)(2,1)S(1)}, bf16[192,1152]{1,0:T(8,128)(2,1)S(1)}, u32[]{:S(2)}, u32[]{:S(2)}) collective-permute-start(bf16[192,1152]{1,0:T(8,128)(2,1)S(1)} %get-tuple-element.217), channel_id=1, source_target_pairs={{0,24},{4,28},{8,16},{12,20},{16,8},{20,12},{24,0},{28,4},{1,25},{... | collective-permute-start | bytes 1327112 | tf_op jit(solution)/shard_map/ppermute | solution.py:388
  181.5 50.1 %collective-permute-start.25 = (bf16[192,1152]{1,0:T(8,128)(2,1)S(1)}, bf16[192,1152]{1,0:T(8,128)(2,1)S(1)}, u32[]{:S(2)}, u32[]{:S(2)}) collective-permute-start(bf16[192,1152]{1,0:T(8,128)(2,1)S(1)} %get-tuple-element.216), channel_id=1, source_target_pairs={{0,28},{4,24},{8,20},{12,16},{16,12},{20,8},{24,4},{28,0},{1,29},{... | collective-permute-start | bytes 1327112 | tf_op jit(solution)/shard_map/ppermute | solution.py:388
  186.5 45.1 %collective-permute-start.26 = (bf16[192,1152]{1,0:T(8,128)(2,1)S(1)}, bf16[192,1152]{1,0:T(8,128)(2,1)S(1)}, u32[]{:S(2)}, u32[]{:S(2)}) collective-permute-start(bf16[192,1152]{1,0:T(8,128)(2,1)S(1)} %get-tuple-element.215), channel_id=1, source_target_pairs={{0,8},{4,12},{8,0},{12,4},{16,24},{20,28},{24,16},{28,20},{1,9},{5... | collective-permute-start | bytes 1327112 | tf_op jit(solution)/shard_map/ppermute | solution.py:388
  423.2 172.9 %reduce-scatter.7.cloned.1.call-start = ((), (), s32[]{:S(2)}) async-start(), calls=%async_computation.9 | async-start | bytes 3194880 | tf_op jit(solution)/shard_map/reduce_scatter | solution.py:744
  437.8 36.3 %collective-permute-start.65 = (bf16[192,1152]{1,0:T(8,128)(2,1)}, bf16[192,1152]{1,0:T(8,128)(2,1)}, u32[]{:S(2)}, u32[]{:S(2)}) collective-permute-start(bf16[192,1152]{1,0:T(8,128)(2,1)} %get-tuple-element.209), channel_id=1, source_target_pairs={{0,4},{4,0},{8,12},{12,8},{16,20},{20,16},{24,28},{28,24},{1,5},{5... | collective-permute-start | bytes 1327112 | tf_op jit(solution)/shard_map/ppermute | solution.py:388
  438.1 36.2 %collective-permute-start.66 = (bf16[192,1152]{1,0:T(8,128)(2,1)}, bf16[192,1152]{1,0:T(8,128)(2,1)}, u32[]{:S(2)}, u32[]{:S(2)}) collective-permute-start(bf16[192,1152]{1,0:T(8,128)(2,1)} %get-tuple-element.208), channel_id=1, source_target_pairs={{0,8},{4,12},{8,0},{12,4},{16,24},{20,28},{24,16},{28,20},{1,9},{5... | collective-permute-start | bytes 1327112 | tf_op jit(solution)/shard_map/ppermute | solution.py:388
  472.6 32.3 %collective-permute-start.68 = (bf16[192,1152]{1,0:T(8,128)(2,1)}, bf16[192,1152]{1,0:T(8,128)(2,1)}, u32[]{:S(2)}, u32[]{:S(2)}) collective-permute-start(bf16[192,1152]{1,0:T(8,128)(2,1)} %get-tuple-element.206), channel_id=1, source_target_pairs={{0,16},{4,20},{8,24},{12,28},{16,0},{20,4},{24,8},{28,12},{1,17},{... | collective-permute-start | bytes 1327112 | tf_op jit(solution)/shard_map/ppermute | solution.py:388
  474.1 39.1 %collective-permute-start.69 = (bf16[192,1152]{1,0:T(8,128)(2,1)}, bf16[192,1152]{1,0:T(8,128)(2,1)}, u32[]{:S(2)}, u32[]{:S(2)}) collective-permute-start(bf16[192,1152]{1,0:T(8,128)(2,1)} %get-tuple-element.205), channel_id=1, source_target_pairs={{0,20},{4,16},{8,28},{12,24},{16,4},{20,0},{24,12},{28,8},{1,21},{... | collective-permute-start | bytes 1327112 | tf_op jit(solution)/shard_map/ppermute | solution.py:388
  474.3 38.9 %collective-permute-start.70 = (bf16[192,1152]{1,0:T(8,128)(2,1)}, bf16[192,1152]{1,0:T(8,128)(2,1)}, u32[]{:S(2)}, u32[]{:S(2)}) collective-permute-start(bf16[192,1152]{1,0:T(8,128)(2,1)} %get-tuple-element.204), channel_id=1, source_target_pairs={{0,24},{4,28},{8,16},{12,20},{16,8},{20,12},{24,0},{28,4},{1,25},{... | collective-permute-start | bytes 1327112 | tf_op jit(solution)/shard_map/ppermute | solution.py:388
  476.7 36.4 %collective-permute-start.71 = (bf16[192,1152]{1,0:T(8,128)(2,1)}, bf16[192,1152]{1,0:T(8,128)(2,1)}, u32[]{:S(2)}, u32[]{:S(2)}) collective-permute-start(bf16[192,1152]{1,0:T(8,128)(2,1)} %get-tuple-element.203), channel_id=1, source_target_pairs={{0,28},{4,24},{8,20},{12,16},{16,12},{20,8},{24,4},{28,0},{1,29},{... | collective-permute-start | bytes 1327112 | tf_op jit(solution)/shard_map/ppermute | solution.py:388
  484.4 33.6 %collective-permute-start.73 = (f32[2,8,1536]{2,1,0:T(8,128)S(1)}, f32[2,8,1536]{2,1,0:T(8,128)S(1)}, u32[]{:S(2)}, u32[]{:S(2)}) collective-permute-start(f32[2,8,1536]{2,1,0:T(8,128)S(1)} %fusion.96), channel_id=1, source_target_pairs={{0,2},{1,3},{2,0},{3,1},{4,6},{5,7},{6,4},{7,5},{8,10},{9,11},{10,... | collective-permute-start | bytes 294920 | tf_op jit(solution)/shard_map/ppermute | solution.py:388
  519.9 123.1 %reduce-scatter.11.cloned.1.call-start = ((), (), s32[]{:S(2)}) async-start(), calls=%async_computation.11 | async-start | bytes 1474560 | tf_op jit(solution)/shard_map/reduce_scatter | solution.py:785
  536.3 149.5 %reduce-scatter.9.cloned.1.call-start = ((), (), s32[]{:S(2)}) async-start(), calls=%async_computation.10 | async-start | bytes 3194880 | tf_op jit(solution)/shard_map/reduce_scatter | solution.py:744
  543.3 39.1 %collective-permute-start.81 = (bf16[192,1152]{1,0:T(8,128)(2,1)}, bf16[192,1152]{1,0:T(8,128)(2,1)}, u32[]{:S(2)}, u32[]{:S(2)}) collective-permute-start(bf16[192,1152]{1,0:T(8,128)(2,1)} %get-tuple-element.197), channel_id=1, source_target_pairs={{0,20},{4,16},{8,28},{12,24},{16,4},{20,0},{24,12},{28,8},{1,21},{... | collective-permute-start | bytes 1327112 | tf_op jit(solution)/shard_map/ppermute | solution.py:388
  550.0 36.9 %collective-permute-start.82 = (bf16[192,1152]{1,0:T(8,128)(2,1)}, bf16[192,1152]{1,0:T(8,128)(2,1)}, u32[]{:S(2)}, u32[]{:S(2)}) collective-permute-start(bf16[192,1152]{1,0:T(8,128)(2,1)} %get-tuple-element.196), channel_id=1, source_target_pairs={{0,24},{4,28},{8,16},{12,20},{16,8},{20,12},{24,0},{28,4},{1,25},{... | collective-permute-start | bytes 1327112 | tf_op jit(solution)/shard_map/ppermute | solution.py:388
  553.2 33.7 %collective-permute-start.83 = (bf16[192,1152]{1,0:T(8,128)(2,1)}, bf16[192,1152]{1,0:T(8,128)(2,1)}, u32[]{:S(2)}, u32[]{:S(2)}) collective-permute-start(bf16[192,1152]{1,0:T(8,128)(2,1)} %get-tuple-element.195), channel_id=1, source_target_pairs={{0,28},{4,24},{8,20},{12,16},{16,12},{20,8},{24,4},{28,0},{1,29},{... | collective-permute-start | bytes 1327112 | tf_op jit(solution)/shard_map/ppermute | solution.py:388
  561.7 28.0 %collective-permute-start.75 = (bf16[256,768]{1,0:T(8,128)(2,1)}, bf16[256,768]{1,0:T(8,128)(2,1)}, u32[]{:S(2)}, u32[]{:S(2)}) collective-permute-start(bf16[256,768]{1,0:T(8,128)(2,1)} %get-tuple-element.232), channel_id=1, source_target_pairs={{0,8},{4,12},{8,0},{12,4},{16,24},{20,28},{24,16},{28,20},{1,9},{5... | collective-permute-start | bytes 1179656 | tf_op jit(solution)/shard_map/ppermute | solution.py:388
  562.9 28.4 %collective-permute-start.76 = (bf16[256,768]{1,0:T(8,128)(2,1)}, bf16[256,768]{1,0:T(8,128)(2,1)}, u32[]{:S(2)}, u32[]{:S(2)}) collective-permute-start(bf16[256,768]{1,0:T(8,128)(2,1)} %get-tuple-element.231), channel_id=1, source_target_pairs={{0,16},{4,20},{8,24},{12,28},{16,0},{20,4},{24,8},{28,12},{1,17},{... | collective-permute-start | bytes 1179656 | tf_op jit(solution)/shard_map/ppermute | solution.py:388
  641.3 42.3 %collective-permute-start.86 = (bf16[128,1536]{1,0:T(8,128)(2,1)}, bf16[128,1536]{1,0:T(8,128)(2,1)S(1)}, u32[]{:S(2)}, u32[]{:S(2)}) collective-permute-start(bf16[128,1536]{1,0:T(8,128)(2,1)} %add_convert_fusion), channel_id=1, source_target_pairs={{0,0},{4,1},{8,2},{12,3},{3,4},{7,5},{11,6},{15,7},{1,8},{5,9},{9,... | collective-permute-start | bytes 1179656 | tf_op jit(solution)/shard_map/ppermute | solution.py:612
  644.0 39.0 %collective-permute-start.91 = (f32[1,12,128]{2,1,0:T(8,128)S(1)}, f32[1,12,128]{2,1,0:T(8,128)S(1)}, u32[]{:S(2)}, u32[]{:S(2)}) collective-permute-start(f32[1,12,128]{2,1,0:T(8,128)S(1)} %add.476), channel_id=1, source_target_pairs={{0,2},{1,3},{2,0},{3,1},{4,6},{5,7},{6,4},{7,5},{8,10},{9,11},{10,... | collective-permute-start | bytes 18440 | tf_op jit(solution)/shard_map/ppermute | solution.py:388
  (139 other events, 1779.4 us)
Sparse Core Ops, SparseCore 0:
  10.2 63.4 all-gather.4
  75.8 54.1 all-gather.6
  131.6 29.0 all-gather.8
  166.3 41.0 all-gather.10
  423.4 27.5 reduce-scatter.4
  520.0 51.2 reduce-scatter.6
  574.2 38.4 reduce-scatter.10
  615.0 64.9 reduce-scatter.8
